TPU v7x, 512 devices: a whole 4x8x8 slice. The times are simulated.
512 devices in a mesh: tor: 8 (over z_lo, x), pol: 64 (over y, z_hi, core).
Axes of the slice: x: 4, y: 8, z: 8 (z_hi: 4, z_lo: 2; z = z_hi * 2 + z_lo), core: 2. Of those that a mesh axis runs over, the one named last changes fastest.
Arguments:
- plasma_state: float32 [6, 8, 512, 256], P(None, 'tor', 'pol'), may hold values from -3 to 3
- right_side: float32 [6, 8, 512, 256], P(None, 'tor', 'pol'), may hold values from -12 to 12
- resistivity: float32 [8, 512, 256], P('tor', 'pol'), may hold values from 0.05 to 0.6
- jacobi_blocks: float32 [6, 6, 8, 512, 256], P(None, None, 'tor', 'pol'), may hold values from -0.6 to 1.6, as said below
Outputs:
- update: float32 [6, 8, 512, 256], P(None, 'tor', 'pol')
- estimates: float32 [3], replicated
Inputs may be any that keep to these rules, and one draw needn't show every extreme that they name: `jacobi_blocks`: each block's diagonal entries lie in 0.4 to 1.6.
All inputs are finite; a program needn't handle non-finite values.
Results may differ from a plain program's by a relative error of at most 0.006.
Values may be sent and summed in bfloat16 or wider, within the bound.
A program may use at most 64 MiB of HBM per device.

v0:
```python
import jax
import jax.numpy as jnp
from jax import lax
from jax.sharding import PartitionSpec as P

ITERS = 3


inverse_step = 1.0
viscosity = 0.2
epsilon = 1e-06


def padded_2(cells, sides, width, closed):
    for axis, dim in sides:
        count = lax.axis_size(axis)
        ends = count if closed else count - 1
        head = lax.slice_in_dim(cells, 0, width, axis=dim)
        tail = lax.slice_in_dim(cells, cells.shape[dim] - width, cells.shape[dim], axis=dim)
        cells = jnp.concatenate(
            [
                lax.ppermute(tail, axis, [(i, (i + 1) % count) for i in range(ends)]),
                cells,
                lax.ppermute(head, axis, [((i + 1) % count, i) for i in range(ends)]),
            ],
            axis=dim,
        )
    return cells


def neighbour(values, array_axis, offset):
    length = values.shape[array_axis]
    widths = [(0, 0)] * values.ndim
    widths[array_axis] = (1, 1)
    padded = jnp.pad(values, widths)
    return lax.slice_in_dim(padded, 1 + offset, 1 + offset + length, axis=array_axis)


def linear_flux(plasma, tangent, direction):
    magnetic = plasma[0:3]
    velocity = plasma[3:6]
    tang_mag = tangent[0:3]
    tang_vel = tangent[3:6]
    pressure = jnp.sum(magnetic * tang_mag, axis=0)
    components = []
    for inner_index in range(3):
        components.append(
            tang_vel[direction] * magnetic[inner_index]
            + velocity[direction] * tang_mag[inner_index]
            - tang_mag[direction] * velocity[inner_index]
            - magnetic[direction] * tang_vel[inner_index]
        )
    for inner_index in range(3):
        moment = (
            tang_vel[direction] * velocity[inner_index]
            + velocity[direction] * tang_vel[inner_index]
            - tang_mag[direction] * magnetic[inner_index]
            - magnetic[direction] * tang_mag[inner_index]
        )
        if inner_index == direction:
            moment = moment + pressure
        components.append(moment)
    return jnp.stack(components)


def diffusion_field(resistivity):
    shape = (3,) + resistivity.shape
    return jnp.concatenate(
        [jnp.broadcast_to(resistivity[None], shape), jnp.full(shape, viscosity, jnp.float32)]
    )


def jacobian_product(
    plasma, tangent, plasma_planes, tangent_planes, plasma_rows, tangent_rows, diffusion
):
    result_sum = inverse_step * tangent
    flux_planes = linear_flux(plasma_planes, tangent_planes, 0)
    result_sum = result_sum + 0.5 * (flux_planes[:, 2:] - flux_planes[:, :-2])
    laplace_sum = tangent_planes[:, 2:] + tangent_planes[:, :-2] - 2.0 * tangent
    flux_rows = linear_flux(plasma_rows, tangent_rows, 1)
    result_sum = result_sum + 0.5 * (flux_rows[:, :, 2:] - flux_rows[:, :, :-2])
    laplace_sum = laplace_sum + tangent_rows[:, :, 2:] + tangent_rows[:, :, :-2] - 2.0 * tangent
    flux_depth = linear_flux(plasma, tangent, 2)
    result_sum = result_sum + 0.5 * (neighbour(flux_depth, 3, 1) - neighbour(flux_depth, 3, -1))
    laplace_sum = laplace_sum + neighbour(tangent, 3, 1) + neighbour(tangent, 3, -1) - 2.0 * tangent
    return result_sum - diffusion * laplace_sum


def precondition(blocks, vector):
    widened = vector.astype(jnp.float32)
    total = blocks[:, 0] * widened[0]
    for column in range(1, 6):
        total = total + blocks[:, column] * widened[column]
    return total


def least_squares(columns, initial_norm):
    count = len(columns)
    rhs_list = [initial_norm] + [jnp.float32(0.0)] * count
    cosines = []
    sines = []
    triangle = []
    estimate_list = []
    for column in range(count):
        entries = list(columns[column])
        for inner_index in range(column):
            first_value = entries[inner_index]
            second_value = entries[inner_index + 1]
            entries[inner_index] = (
                cosines[inner_index] * first_value + sines[inner_index] * second_value
            )
            entries[inner_index + 1] = (
                -sines[inner_index] * first_value + cosines[inner_index] * second_value
            )
        first_value = entries[column]
        second_value = entries[column + 1]
        radius = jnp.sqrt(first_value * first_value + second_value * second_value)
        cosine = first_value / radius
        sine_value = second_value / radius
        cosines.append(cosine)
        sines.append(sine_value)
        entries[column] = radius
        triangle.append(entries[: column + 1])
        previous = rhs_list[column]
        rhs_list[column] = cosine * previous
        rhs_list[column + 1] = -sine_value * previous
        estimate_list.append(jnp.abs(rhs_list[column + 1]))
    weights = [jnp.float32(0.0)] * count
    for column in reversed(range(count)):
        partial_value = rhs_list[column]
        for later in range(column + 1, count):
            partial_value = partial_value - triangle[later][column] * weights[later]
        weights[column] = partial_value / triangle[column][column]
    return (weights, estimate_list)


def shards(plasma_state, right_side, resistivity, jacobi_blocks):
    cell_count = (
        6
        * plasma_state.shape[1]
        * plasma_state.shape[2]
        * plasma_state.shape[3]
        * lax.axis_size("tor")
        * lax.axis_size("pol")
    )
    diffusion = diffusion_field(resistivity)
    plasma_planes = padded_2(plasma_state.astype(jnp.bfloat16), (("tor", 1),), 1, True).astype(
        plasma_state.dtype
    )
    plasma_rows = padded_2(plasma_state, (("pol", 2),), 1, False)
    square_sum = lax.psum(jnp.sum(right_side * right_side), ("tor", "pol"))
    initial_norm = jnp.sqrt(square_sum + epsilon)
    krylov_basis = [(right_side / initial_norm).astype(jnp.bfloat16)]
    directions = []
    columns = []
    for column in range(ITERS):
        vector = krylov_basis[column]
        tangent = precondition(jacobi_blocks, vector)
        tangent_planes = padded_2(tangent.astype(jnp.bfloat16), (("tor", 1),), 1, True).astype(
            tangent.dtype
        )
        tangent_rows = padded_2(tangent, (("pol", 2),), 1, False)
        image = jacobian_product(
            plasma_state,
            tangent,
            plasma_planes,
            tangent_planes,
            plasma_rows,
            tangent_rows,
            diffusion,
        )
        directions.append(tangent)
        local_products = jnp.stack(
            [jnp.sum(image * earlier.astype(jnp.float32)) for earlier in krylov_basis]
        )
        products = lax.psum(local_products, ("tor", "pol"))
        coefficients = [products[inner_index] for inner_index in range(column + 1)]
        remainder = image
        for inner_index in range(column + 1):
            remainder = remainder - coefficients[inner_index] * krylov_basis[inner_index].astype(
                jnp.float32
            )
        remainder_square = lax.psum(jnp.sum(remainder * remainder), ("tor", "pol"))
        new_norm = jnp.sqrt(remainder_square + epsilon)
        columns.append(coefficients + [new_norm])
        if column + 1 < ITERS:
            krylov_basis.append((remainder / new_norm).astype(jnp.bfloat16))
    weights, estimate_list = least_squares(columns, initial_norm)
    update = weights[0] * directions[0]
    for column in range(1, ITERS):
        update = update + weights[column] * directions[column]
    estimates = jnp.stack(estimate_list) / jnp.sqrt(jnp.float32(cell_count))
    return (update, estimates)


def solution(mesh):
    return jax.shard_map(
        shards,
        mesh=mesh,
        in_specs=(
            P(None, "tor", "pol", None),
            P(None, "tor", "pol", None),
            P("tor", "pol", None),
            P(None, None, "tor", "pol", None),
        ),
        out_specs=(P(None, "tor", "pol", None), P()),
        check_vma=False,
    )
```

profile of v0, /device:TPU:1, one launch (start us, length us, event | category | flops | bytes accessed | tf_op | source)
XLA Modules:
  0.0 785.8 jit_solution(5154822776508504955)
XLA Ops:
  0.6 1.5 multiply_reduce_fusion.5
  2.1 106.1 %psum.49 = f32[]{:T(128)} all-reduce(f32[]{:T(128)} %multiply_reduce_fusion.5), channel_id=1, replica_groups=mesh['tor'=8,'pol'=64] {'tor','pol'}, use_global_device_ids=true, to_apply=%region_1.0 | all-reduce | flops 1 | bytes 8 | tf_op jit(solution)/shard_map/psum | solution.py:151
  108.9 0.0 copy-start
  108.9 1.0 fusion.104
  109.9 2.5 collective-permute-start
  112.4 4.9 collective-permute-start.1
  117.3 1.9 collective-permute-start.2
  119.3 3.0 collective-permute-start.4
  122.3 1.9 collective-permute-start.5
  124.3 4.5 collective-permute-start.6
  128.9 1.9 collective-permute-start.7
  130.9 5.8 collective-permute-start.3
  136.8 0.0 collective-permute-done.1
  136.9 0.0 collective-permute-done.2
  136.9 0.7 collective-permute-done.3
  137.7 0.0 copy-start.3
  137.7 0.7 copy-done.3
  138.4 0.7 fusion.3
  139.1 104.8 %psum.50 = f32[]{:T(128)} all-reduce(f32[]{:T(128)} %get-tuple-element.15), channel_id=1, replica_groups=mesh['tor'=8,'pol'=64] {'tor','pol'}, use_global_device_ids=true, to_apply=%region_6.7 | all-reduce | flops 1 | bytes 8 | tf_op jit(solution)/shard_map/psum | solution.py:176
  243.9 1.3 multiply_reduce_fusion.4
  245.2 95.1 %psum.51 = f32[]{:T(128)} all-reduce(f32[]{:T(128)} %multiply_reduce_fusion.4), channel_id=1, replica_groups=mesh['tor'=8,'pol'=64] {'tor','pol'}, use_global_device_ids=true, to_apply=%region_8.9 | all-reduce | flops 1 | bytes 8 | tf_op jit(solution)/shard_map/psum | solution.py:183
  341.0 0.7 fusion.102
  341.7 3.7 collective-permute-start.8
  345.4 3.7 collective-permute-start.9
  349.2 3.1 collective-permute-start.10
  352.3 1.9 collective-permute-start.11
  356.3 0.0 collective-permute-done.10
  356.3 1.8 collective-permute-done.11
  358.5 0.7 fusion.5
  359.2 1.4 pad_maximum_fusion.10
  360.6 101.5 %psum.52 = f32[2]{0:T(128)S(1)} all-reduce(f32[2]{0:T(128)S(1)} %pad_maximum_fusion.10), channel_id=1, replica_groups=mesh['tor'=8,'pol'=64] {'tor','pol'}, use_global_device_ids=true, to_apply=%region_14.15 | all-reduce | flops 2 | bytes 16 | tf_op jit(solution)/shard_map/psum | solution.py:176
  462.1 0.6 fusion.112
  462.7 1.9 multiply_reduce_fusion.2
  464.6 95.6 %psum.53 = f32[]{:T(128)} all-reduce(f32[]{:T(128)} %multiply_reduce_fusion.2), channel_id=1, replica_groups=mesh['tor'=8,'pol'=64] {'tor','pol'}, use_global_device_ids=true, to_apply=%region_16.17 | all-reduce | flops 1 | bytes 8 | tf_op jit(solution)/shard_map/psum | solution.py:183
  560.8 1.3 fusion.80
  562.2 2.8 collective-permute-start.12
  565.0 4.6 collective-permute-start.13
  569.6 3.0 collective-permute-start.14
  572.6 1.9 collective-permute-start.15
  577.4 1.1 collective-permute-done.15
  578.8 0.8 fusion.8
  579.6 2.0 pad_maximum_fusion.11
  581.6 99.6 %psum.54 = f32[3]{0:T(128)S(1)} all-reduce(f32[3]{0:T(128)S(1)} %pad_maximum_fusion.11), channel_id=1, replica_groups=mesh['tor'=8,'pol'=64] {'tor','pol'}, use_global_device_ids=true, to_apply=%region_23.24 | all-reduce | flops 3 | bytes 24 | tf_op jit(solution)/shard_map/psum | solution.py:176
  681.2 0.6 fusion.111
  684.4 2.6 fusion.13
  687.6 95.3 %psum.55 = f32[]{:T(128)} all-reduce(f32[]{:T(128)} %fusion.13), channel_id=1, replica_groups=mesh['tor'=8,'pol'=64] {'tor','pol'}, use_global_device_ids=true, to_apply=%region_25.26 | all-reduce | flops 1 | bytes 8 | tf_op jit(solution)/shard_map/psum | solution.py:183
  784.5 0.6 multiply_add_fusion
  785.2 0.6 maximum_multiply_fusion
  (98 shorter events, 1.1 us)
Async XLA Ops:
  0.6 108.3 %copy-start.2 = (f32[6,1,8,256]{3,2,1,0:T(8,128)S(1)}, f32[6,1,8,256]{3,2,1,0:T(8,128)}, u32[]{:S(2)}) copy-start(f32[6,1,8,256]{3,2,1,0:T(8,128)} %param.5) | copy-start | bytes 147460
  108.9 8.4 %copy-start = (f32[6,1,8,256]{3,2,1,0:T(8,128)S(1)}, f32[6,1,8,256]{3,2,1,0:T(8,128)}, u32[]{:S(2)}) copy-start(f32[6,1,8,256]{3,2,1,0:T(8,128)} %param.4) | copy-start | bytes 147460
  109.9 26.9 %collective-permute-start = (bf16[6,1,8,256]{3,2,1,0:T(8,128)(2,1)S(1)}, bf16[6,1,8,256]{3,2,1,0:T(8,128)(2,1)S(1)}, u32[]{:S(2)}, u32[]{:S(2)}) collective-permute-start(bf16[6,1,8,256]{3,2,1,0:T(8,128)(2,1)S(1)} %get-tuple-element.17), channel_id=1, source_target_pairs={{0,64},{64,128},{128,192},{192,256},{256,320},{320,384},{384,448},... | collective-permute-start | bytes 73736 | tf_op jit(solution)/shard_map/ppermute | solution.py:22
  112.4 24.4 %collective-permute-start.1 = (bf16[6,1,8,256]{3,2,1,0:T(8,128)(2,1)S(1)}, bf16[6,1,8,256]{3,2,1,0:T(8,128)(2,1)S(1)}, u32[]{:S(2)}, u32[]{:S(2)}) collective-permute-start(bf16[6,1,8,256]{3,2,1,0:T(8,128)(2,1)S(1)} %get-tuple-element.17), channel_id=1, source_target_pairs={{64,0},{128,64},{192,128},{256,192},{320,256},{384,320},{448,384},... | collective-permute-start | bytes 73736 | tf_op jit(solution)/shard_map/ppermute | solution.py:24
  117.3 19.5 %collective-permute-start.2 = (bf16[6,1,8,256]{3,2,1,0:T(8,128)(2,1)S(1)}, bf16[6,1,8,256]{3,2,1,0:T(8,128)(2,1)S(1)}, u32[]{:S(2)}, u32[]{:S(2)}) collective-permute-start(bf16[6,1,8,256]{3,2,1,0:T(8,128)(2,1)S(1)} %convert_element_type.95), channel_id=1, source_target_pairs={{0,64},{64,128},{128,192},{192,256},{256,320},{320,384},{384,448},... | collective-permute-start | bytes 73736 | tf_op jit(solution)/shard_map/ppermute | solution.py:22
  119.3 5.1 collective-permute-start.4
  122.3 6.6 collective-permute-start.5
  124.3 6.5 collective-permute-start.6
  128.9 7.7 collective-permute-start.7
  130.9 6.7 collective-permute-start.3
  137.7 0.7 copy-start.3
  139.1 202.6 %copy-start.1 = (f32[6,6,1,8,256]{4,3,2,1,0:T(8,128)S(1)}, f32[6,6,1,8,256]{4,3,2,1,0:T(8,128)}, u32[]{:S(2)}) copy-start(f32[6,6,1,8,256]{4,3,2,1,0:T(8,128)} %param.7) | copy-start | bytes 884740
  341.7 16.6 %collective-permute-start.8 = (bf16[6,1,8,256]{3,2,1,0:T(8,128)(2,1)S(1)}, bf16[6,1,8,256]{3,2,1,0:T(8,128)(2,1)S(1)}, u32[]{:S(2)}, u32[]{:S(2)}) collective-permute-start(bf16[6,1,8,256]{3,2,1,0:T(8,128)(2,1)S(1)} %get-tuple-element.11), channel_id=1, source_target_pairs={{0,64},{64,128},{128,192},{192,256},{256,320},{320,384},{384,448},... | collective-permute-start | bytes 73736 | tf_op jit(solution)/shard_map/ppermute | solution.py:22
  345.4 12.9 %collective-permute-start.9 = (bf16[6,1,8,256]{3,2,1,0:T(8,128)(2,1)S(1)}, bf16[6,1,8,256]{3,2,1,0:T(8,128)(2,1)S(1)}, u32[]{:S(2)}, u32[]{:S(2)}) collective-permute-start(bf16[6,1,8,256]{3,2,1,0:T(8,128)(2,1)S(1)} %get-tuple-element.11), channel_id=1, source_target_pairs={{64,0},{128,64},{192,128},{256,192},{320,256},{384,320},{448,384},... | collective-permute-start | bytes 73736 | tf_op jit(solution)/shard_map/ppermute | solution.py:24
  349.2 7.2 collective-permute-start.10
  352.3 5.8 collective-permute-start.11
  562.2 16.5 %collective-permute-start.12 = (bf16[6,1,8,256]{3,2,1,0:T(8,128)(2,1)S(1)}, bf16[6,1,8,256]{3,2,1,0:T(8,128)(2,1)S(1)}, u32[]{:S(2)}, u32[]{:S(2)}) collective-permute-start(bf16[6,1,8,256]{3,2,1,0:T(8,128)(2,1)S(1)} %get-tuple-element.8), channel_id=1, source_target_pairs={{0,64},{64,128},{128,192},{192,256},{256,320},{320,384},{384,448},... | collective-permute-start | bytes 73736 | tf_op jit(solution)/shard_map/ppermute | solution.py:22
  565.0 13.7 %collective-permute-start.13 = (bf16[6,1,8,256]{3,2,1,0:T(8,128)(2,1)S(1)}, bf16[6,1,8,256]{3,2,1,0:T(8,128)(2,1)S(1)}, u32[]{:S(2)}, u32[]{:S(2)}) collective-permute-start(bf16[6,1,8,256]{3,2,1,0:T(8,128)(2,1)S(1)} %get-tuple-element.8), channel_id=1, source_target_pairs={{64,0},{128,64},{192,128},{256,192},{320,256},{384,320},{448,384},... | collective-permute-start | bytes 73736 | tf_op jit(solution)/shard_map/ppermute | solution.py:24
  569.6 7.7 collective-permute-start.14
  572.6 5.8 collective-permute-start.15
where the time goes:
time: 787 us; the launch traced here: 786 us
  blocking collectives  698 us (89%)
  starting transfers between devices  51.1 us (6%)
  other arithmetic  18 us (2%)
  between operations  13.1 us (2%)
    psum x3, blocking collectives, shards(): products = lax.psum(local_products, ('tor', 'pol'))  306 us
    psum x3, blocking collectives, shards(): remainder_square = lax.psum(jnp.sum(remainder * remainder), ('tor', 'pol'))  286 us
    psum x1, blocking collectives, shards(): square_sum = lax.psum(jnp.sum(right_side * right_side), ('tor', 'pol'))  106 us
    ppermute x8, starting transfers between devices, padded_2(): lax.ppermute(head, axis, [((i + 1) % count, i) for i in range(ends)])  26.7 us
    ppermute x8, starting transfers between devices, padded_2(): lax.ppermute(tail, axis, [(i, (i + 1) % count) for i in range(ends)])  24.5 us
  transfers between devices with their start and end apart: 16, of which 3 were waited for; matrix products, arithmetic and copies ran while one was open for 0% of the time, Pallas kernels for 0%

commit v1 on v0

v1 whole, which is shorter than its diff:
```python
import functools

import jax
import jax.numpy as jnp
from jax import lax
from jax.experimental import pallas as pl
from jax.experimental.pallas import tpu as pltpu
from jax.sharding import PartitionSpec as P

ITERS = 3
inverse_step = 1.0
viscosity = 0.2
epsilon = 1e-06

MESH = pl.DeviceIdType.MESH
F32 = jnp.float32
BF16 = jnp.bfloat16
PAIRS = [(i, j) for j in range(ITERS + 1) for i in range(j + 1)]
GROUP = 8


def flux(p, t, k):
    B, V, b, w = p[0:3], p[3:6], t[0:3], t[3:6]
    parts = []
    for i in range(3):
        parts.append(None if i == k else w[k] * B[i] + V[k] * b[i] - b[k] * V[i] - B[k] * w[i])
    for i in range(3):
        moment = w[k] * V[i] + V[k] * w[i] - b[k] * B[i] - B[k] * b[i]
        if i == k:
            moment = moment + (B[0] * b[0] + B[1] * b[1] + B[2] * b[2])
        parts.append(moment)
    return parts


def small_solve(gram, like):
    count = ITERS
    zero = jnp.zeros_like(like)
    norm0 = jnp.sqrt(gram[0][0] + epsilon)
    coefs = [[1.0 / norm0]]
    columns = []
    for j in range(count):
        shifted = [None] + coefs[j]
        size = j + 2
        applied = []
        for row in range(size):
            total = None
            for col in range(1, size):
                term = gram[row][col] * shifted[col]
                total = term if total is None else total + term
            applied.append(total)
        column = []
        for i in range(j + 1):
            total = None
            for row in range(i + 1):
                term = coefs[i][row] * applied[row]
                total = term if total is None else total + term
            column.append(total)
        remainder = []
        for row in range(size):
            total = shifted[row]
            for i in range(j + 1):
                if row <= i:
                    term = column[i] * coefs[i][row]
                    total = -term if total is None else total - term
            remainder.append(total)
        square = None
        for row in range(size):
            inner = None
            for col in range(size):
                term = gram[row][col] * remainder[col]
                inner = term if inner is None else inner + term
            term = inner * remainder[row]
            square = term if square is None else square + term
        norm = jnp.sqrt(jnp.maximum(square, 0.0) + epsilon)
        columns.append(column + [norm])
        if j + 1 < count:
            inverse = 1.0 / norm
            coefs.append([entry * inverse for entry in remainder])
    rhs = [norm0] + [zero] * count
    cosines, sines, triangle, estimates = [], [], [], []
    for column in range(count):
        entries = list(columns[column])
        for i in range(column):
            first, second = entries[i], entries[i + 1]
            entries[i] = cosines[i] * first + sines[i] * second
            entries[i + 1] = cosines[i] * second - sines[i] * first
        first, second = entries[column], entries[column + 1]
        radius = jnp.sqrt(first * first + second * second)
        inverse = 1.0 / radius
        cosine, sine = first * inverse, second * inverse
        cosines.append(cosine)
        sines.append(sine)
        triangle.append(entries[:column] + [inverse])
        previous = rhs[column]
        rhs[column] = cosine * previous
        rhs[column + 1] = -sine * previous
        estimates.append(jnp.abs(rhs[column + 1]))
    weights = [zero] * count
    for column in reversed(range(count)):
        value = rhs[column]
        for later in range(column + 1, count):
            value = value - triangle[later][column] * weights[later]
        weights[column] = value * triangle[column][column]
    alphas = []
    for row in range(count):
        total = None
        for j in range(row, count):
            term = weights[j] * coefs[j][row]
            total = term if total is None else total + term
        alphas.append(total)
    return alphas, estimates


def kernel(sizes, cell_count, plasma_hbm, right_hbm, resist_hbm, blocks_hbm, update_ref, est_ref,
           plasma, right, resist, blocks, w_ref, t_ref, up_ref, down_ref,
           tor_tx, tor_rx, pol_tx, pol_rx, sums,
           load_sem, tor_send, tor_recv, pol_send, pol_recv, sum_send, sum_recv):
    tors, pols = sizes
    tor = lax.axis_index("tor")
    pol = lax.axis_index("pol")
    tor_next, tor_prev = lax.rem(tor + 1, tors), lax.rem(tor + tors - 1, tors)
    pol_next, pol_prev = lax.rem(pol + 1, pols), lax.rem(pol + pols - 1, pols)
    outer, inner = pol // GROUP, lax.rem(pol, GROUP)

    def in_group(stage, rank):
        if stage == 0:
            return {"tor": rank, "pol": pol}
        if stage == 1:
            return {"tor": tor, "pol": outer * GROUP + rank}
        return {"tor": tor, "pol": rank * GROUP + inner}

    ranks = [tor, inner, outer]
    counts = [tors, GROUP, pols // GROUP]

    barrier = pltpu.get_barrier_semaphore()
    greeted = 0
    for stage in range(3):
        for step in range(1, counts[stage]):
            partner = lax.rem(ranks[stage] + step, counts[stage])
            pl.semaphore_signal(barrier, inc=1, device_id=in_group(stage, partner), device_id_type=MESH)
            greeted += 1
    for neighbour in (pol_next, pol_prev):
        pl.semaphore_signal(barrier, inc=1, device_id={"tor": tor, "pol": neighbour}, device_id_type=MESH)
        greeted += 1

    loads = [
        pltpu.make_async_copy(plasma_hbm, plasma, load_sem.at[0]),
        pltpu.make_async_copy(right_hbm, right, load_sem.at[1]),
        pltpu.make_async_copy(resist_hbm, resist, load_sem.at[2]),
    ]
    for row in range(6):
        loads.append(
            pltpu.make_async_copy(
                blocks_hbm.at[pl.ds(6 * row, 6)], blocks.at[pl.ds(6 * row, 6)], load_sem.at[3 + row]
            )
        )
    for load in loads:
        load.start()

    lane = lax.broadcasted_iota(jnp.int32, (8, 256), 1)
    sub = lax.broadcasted_iota(jnp.int32, (8, 256), 0)

    def up_depth(x):
        return jnp.where(lane == 255, 0.0, pltpu.roll(x, 255, 1))

    def down_depth(x):
        return jnp.where(lane == 0, 0.0, pltpu.roll(x, 1, 1))

    def up_row(x, halo):
        return jnp.where(sub == 7, jnp.broadcast_to(halo, (8, 256)), pltpu.roll(x, 7, 0))

    def down_row(x, halo):
        return jnp.where(sub == 0, jnp.broadcast_to(halo, (8, 256)), pltpu.roll(x, 1, 0))

    def tor_copies(slot):
        return [
            pltpu.make_async_remote_copy(
                src_ref=tor_tx.at[slot],
                dst_ref=tor_rx.at[slot, way],
                send_sem=tor_send.at[slot, way],
                recv_sem=tor_recv.at[slot, way],
                device_id={"tor": (tor_next, tor_prev)[way], "pol": pol},
                device_id_type=MESH,
            )
            for way in range(2)
        ]

    def pol_copies(slot):
        return [
            pltpu.make_async_remote_copy(
                src_ref=pol_tx.at[slot, way],
                dst_ref=pol_rx.at[slot, way],
                send_sem=pol_send.at[slot, way],
                recv_sem=pol_recv.at[slot, way],
                device_id={"tor": tor, "pol": (pol_next, pol_prev)[way]},
                device_id_type=MESH,
            )
            for way in range(2)
        ]

    def pack(slot, x):
        for c in range(6):
            pol_tx[slot, 0, c : c + 1, :] = x[c][7:8, :]
            pol_tx[slot, 1, c : c + 1, :] = x[c][0:1, :]
        for pair in range(3):
            tor_tx[slot, 16 * pair : 16 * pair + 16, :] = jnp.concatenate(
                [x[2 * pair], x[2 * pair + 1]], axis=0
            ).astype(BF16)

    def from_tor(slot, way):
        planes = []
        for pair in range(3):
            both = tor_rx[slot, way, 16 * pair : 16 * pair + 16, :].astype(F32)
            planes += [both[0:8], both[8:16]]
        return planes

    def precondition(vector):
        result = []
        for a in range(6):
            total = blocks[6 * a] * vector[0]
            for b in range(1, 6):
                total = total + blocks[6 * a + b] * vector[b]
            result.append(total)
        return result

    loads[0].wait()
    pack(3, [plasma[c] for c in range(6)])
    pl.semaphore_wait(barrier, greeted)
    flying = tor_copies(3) + pol_copies(3)
    for copy in flying:
        copy.start()
    for load in loads[1:]:
        load.wait()
    eta = resist[...]

    gram_rows = {}

    def product(i, j):
        total = None
        for c in range(6):
            term = w_ref[i, c] * w_ref[j, c]
            total = term if total is None else total + term
        total = total[:, 0:128] + total[:, 128:256]
        gram_rows[(i, j)] = jnp.sum(total, axis=0, keepdims=True)

    for c in range(6):
        w_ref[0, c] = right[c]

    for k in range(ITERS):
        t = precondition([w_ref[k, c] for c in range(6)])
        for c in range(6):
            t_ref[k, c] = t[c]
        pack(k, t)
        tor_moves, pol_moves = tor_copies(k), pol_copies(k)
        for copy in pol_moves + tor_moves:
            copy.start()
        flying += pol_moves + tor_moves
        p = [plasma[c] for c in range(6)]
        f = flux(p, t, 2)
        partial = []
        for c in range(6):
            coefficient = eta if c < 3 else viscosity
            total = inverse_step * t[c] + coefficient * (6.0 * t[c] - up_depth(t[c]) - down_depth(t[c]))
            if f[c] is not None:
                half = 0.5 * f[c]
                total = total + (up_depth(half) - down_depth(half))
            partial.append(total)
        for i in range(k + 1):
            product(i, k)
        if k == 0:
            for copy in flying[0:4]:
                copy.wait_recv()
            for c in range(6):
                up_ref[c] = up_row(plasma[c], pol_rx[3, 1, c : c + 1, :])
                down_ref[c] = down_row(plasma[c], pol_rx[3, 0, c : c + 1, :])
        for copy in pol_moves:
            copy.wait_recv()
        t_up = [
            up_row(t[c], jnp.where(pol == pols - 1, 0.0, pol_rx[k, 1, c : c + 1, :])) for c in range(6)
        ]
        t_down = [down_row(t[c], jnp.where(pol == 0, 0.0, pol_rx[k, 0, c : c + 1, :])) for c in range(6)]
        f_up = flux([up_ref[c] for c in range(6)], t_up, 1)
        f_down = flux([down_ref[c] for c in range(6)], t_down, 1)
        for c in range(6):
            coefficient = eta if c < 3 else viscosity
            partial[c] = partial[c] - coefficient * (t_up[c] + t_down[c])
            if f_up[c] is not None:
                partial[c] = partial[c] + 0.5 * (f_up[c] - f_down[c])
        for copy in tor_moves:
            copy.wait_recv()
        t_up, t_down = from_tor(k, 1), from_tor(k, 0)
        f_up = flux(from_tor(3, 1), t_up, 0)
        f_down = flux(from_tor(3, 0), t_down, 0)
        for c in range(6):
            coefficient = eta if c < 3 else viscosity
            total = partial[c] - coefficient * (t_up[c] + t_down[c])
            if f_up[c] is not None:
                total = total + 0.5 * (f_up[c] - f_down[c])
            w_ref[k + 1, c] = total

    for i in range(ITERS + 1):
        product(i, ITERS)

    wide_lane = lax.broadcasted_iota(jnp.int32, (16, 128), 1)
    wide_sub = lax.broadcasted_iota(jnp.int32, (16, 128), 0)
    rows = jnp.zeros((16, 128), F32)
    for index, pair in enumerate(PAIRS):
        rows = jnp.where(wide_sub == index, jnp.broadcast_to(gram_rows[pair], (16, 128)), rows)
    rows = jnp.broadcast_to(jnp.sum(rows, axis=1, keepdims=True), (16, 128))
    mine = jnp.sum(jnp.where(wide_lane == wide_sub, rows, 0.0), axis=0, keepdims=True)

    for stage in range(3):
        sums[stage, ranks[stage]] = mine
        moves = []
        for step in range(1, counts[stage]):
            partner = lax.rem(ranks[stage] + step, counts[stage])
            moves.append(
                pltpu.make_async_remote_copy(
                    src_ref=sums.at[stage, ranks[stage]],
                    dst_ref=sums.at[stage, ranks[stage]],
                    send_sem=sum_send.at[stage, step],
                    recv_sem=sum_recv.at[stage, step],
                    device_id=in_group(stage, partner),
                    device_id_type=MESH,
                )
            )
        for copy in moves:
            copy.start()
        flying += moves
        for copy in moves:
            copy.wait_recv()
        mine = sums[stage, 0]
        for rank in range(1, counts[stage]):
            mine = mine + sums[stage, rank]

    row_lane = lax.broadcasted_iota(jnp.int32, (1, 128), 1)
    gram = [[None] * (ITERS + 1) for _ in range(ITERS + 1)]
    for index, (i, j) in enumerate(PAIRS):
        entry = jnp.sum(jnp.where(row_lane == index, mine, 0.0), axis=1, keepdims=True)
        entry = jnp.broadcast_to(entry, (1, 128))
        gram[i][j] = entry
        gram[j][i] = entry
    alphas, estimates = small_solve(gram, gram[0][0])
    scale = 1.0 / float(cell_count) ** 0.5
    est = jnp.zeros((1, 128), F32)
    for index in range(ITERS):
        est = jnp.where(row_lane == index, estimates[index] * scale, est)
    est_ref[...] = est
    full = [jnp.broadcast_to(jnp.concatenate([a, a], axis=1), (8, 256)) for a in alphas]
    for c in range(6):
        update_ref[c] = full[0] * t_ref[0, c] + full[1] * t_ref[1, c] + full[2] * t_ref[2, c]
    for copy in flying:
        copy.wait_send()


def solution(mesh):
    sizes = (mesh.shape["tor"], mesh.shape["pol"])

    def shards(plasma_state, right_side, resistivity, jacobi_blocks):
        cell_count = plasma_state.size * sizes[0] * sizes[1]
        hbm = pl.BlockSpec(memory_space=pl.ANY)
        vmem = pl.BlockSpec(memory_space=pltpu.VMEM)
        update, est = pl.pallas_call(
            functools.partial(kernel, sizes, cell_count),
            out_shape=(jax.ShapeDtypeStruct((6, 8, 256), F32), jax.ShapeDtypeStruct((1, 128), F32)),
            in_specs=[hbm] * 4,
            out_specs=(vmem, vmem),
            scratch_shapes=[
                pltpu.VMEM((6, 8, 256), F32),
                pltpu.VMEM((6, 8, 256), F32),
                pltpu.VMEM((8, 256), F32),
                pltpu.VMEM((36, 8, 256), F32),
                pltpu.VMEM((ITERS + 1, 6, 8, 256), F32),
                pltpu.VMEM((ITERS, 6, 8, 256), F32),
                pltpu.VMEM((6, 8, 256), F32),
                pltpu.VMEM((6, 8, 256), F32),
                pltpu.VMEM((4, 48, 256), BF16),
                pltpu.VMEM((4, 2, 48, 256), BF16),
                pltpu.VMEM((4, 2, 6, 256), F32),
                pltpu.VMEM((4, 2, 6, 256), F32),
                pltpu.VMEM((3, GROUP, 1, 128), F32),
                pltpu.SemaphoreType.DMA((9,)),
                pltpu.SemaphoreType.DMA((4, 2)),
                pltpu.SemaphoreType.DMA((4, 2)),
                pltpu.SemaphoreType.DMA((4, 2)),
                pltpu.SemaphoreType.DMA((4, 2)),
                pltpu.SemaphoreType.DMA((3, GROUP)),
                pltpu.SemaphoreType.DMA((3, GROUP)),
            ],
            compiler_params=pltpu.CompilerParams(collective_id=0, has_side_effects=True),
            name="gmres",
        )(
            plasma_state.reshape(6, 8, 256),
            right_side.reshape(6, 8, 256),
            resistivity.reshape(8, 256),
            jacobi_blocks.reshape(36, 8, 256),
        )
        return update.reshape(6, 1, 8, 256), est[0, :ITERS]

    return jax.shard_map(
        shards,
        mesh=mesh,
        in_specs=(
            P(None, "tor", "pol", None),
            P(None, "tor", "pol", None),
            P("tor", "pol", None),
            P(None, None, "tor", "pol", None),
        ),
        out_specs=(P(None, "tor", "pol", None), P()),
        check_vma=False,
    )
```

time: 787 us -> 44.3 us (0.06)
  blocking collectives: 698 us -> 0 us
  starting transfers between devices: 51.1 us -> 0 us
  Pallas kernels: 0 us -> 40.9 us
  other arithmetic: 18 us -> 0 us
  between operations: 13.1 us -> 0.65 us
    psum x7 -> x0, blocking collectives: 698 us -> none  [the longest x3 306 us: shards(): products = lax.psum(local_products, ('tor', 'pol'))]
    ppermute x16 -> x0, starting transfers between devices: 51.1 us -> none  [the longest x8 26.7 us: padded_2(): lax.ppermute(head, axis, [((i + 1) % count, i) for i in range(ends)])]
    pallas_call x0 -> x1, Pallas kernels: none -> 40.9 us  [shards(): pl.pallas_call(functools.partial(kernel, sizes, cell_count), out_shape=(j...]
    reduce_sum x16 -> x0, other arithmetic: 9.56 us -> none  [the longest x3 5.77 us: shards(): remainder_square = lax.psum(jnp.sum(remainder * remainder), ('tor', 'pol'))]
  transfers between devices with their start and end apart: 16 -> 0, of which waited for: 3 -> 0; matrix products, arithmetic and copies ran while one was open for 0% -> 0% of each run, Pallas kernels for 0% -> 0%
where the time goes in v1:
time: 44.3 us; the launch traced here: 44.1 us
  Pallas kernels  40.9 us (92%)
  local copies, waits for them, and re-layouts  2.53 us (6%)
  between operations  0.65 us (1%)
    pallas_call x1, Pallas kernels, shards(): pl.pallas_call(functools.partial(kernel, sizes, cell_count), out_shape=(j...  40.9 us
    unnamed x3, local copies, waits for them, and re-layouts  2.02 us

profile of v1, /device:TPU:1, one launch (start us, length us, event | category | flops | bytes accessed | tf_op | source)
XLA Modules:
  0.0 44.1 jit_solution(6620688117383828456)
XLA Ops:
  0.6 40.9 %gmres.1 = (f32[6,8,256]{2,1,0:T(8,128)}, f32[1,128]{1,0:T(1,128)}) custom-call(f32[6,8,256]{2,1,0:T(8,128)} %bitcast.10, f32[6,8,256]{2,1,0:T(8,128)} %bitcast.11, f32[8,256]{1,0:T(8,128)} %bitcast.13, f32[36,8,256]{2,1,0:T(8,128)} %bitcast.9), custom_call_target="tpu_custom_call" | custom-call | tf_op jit(solution)/shard_map/gmres/pallas_call | solution.py:363
  41.5 0.0 copy-start
  41.5 0.6 %copy-done = f32[1,128]{1,0:T(1,128)S(1)} copy-done((f32[1,128]{1,0:T(1,128)S(1)}, f32[1,128]{1,0:T(1,128)}, u32[]{:S(2)}) %copy-start) | copy-done | bytes 536
  42.1 0.5 %slice_bitcast_fusion = f32[3]{0:T(128)} fusion(f32[1,128]{1,0:T(1,128)S(1)} %copy-done), kind=kLoop, calls=%fused_computation | loop fusion | bytes 24 | tf_op jit(solution)/shard_map/squeeze | solution.py:398
  42.6 1.4 %copy.8 = f32[6,1,8,256]{3,2,1,0:T(8,128)} copy(f32[6,1,8,256]{3,2,1,0:T(8,128)} %bitcast.12) | data formatting | bytes 98304
Async XLA Ops:
  41.5 0.6 %copy-start = (f32[1,128]{1,0:T(1,128)S(1)}, f32[1,128]{1,0:T(1,128)}, u32[]{:S(2)}) copy-start(f32[1,128]{1,0:T(1,128)} %get-tuple-element.5) | copy-start | bytes 1540

commit v2 on v1

--- a/solution.py
+++ b/solution.py
@@ -111,37 +111,36 @@
     return alphas, estimates
 
 
-def kernel(sizes, cell_count, plasma_hbm, right_hbm, resist_hbm, blocks_hbm, update_ref, est_ref,
-           plasma, right, resist, blocks, w_ref, t_ref, up_ref, down_ref,
-           tor_tx, tor_rx, pol_tx, pol_rx, sums,
-           load_sem, tor_send, tor_recv, pol_send, pol_recv, sum_send, sum_recv):
+def kernel(sizes, plasma_hbm, right_hbm, resist_hbm, blocks_hbm, t_ref, total_ref,
+           plasma, right, resist, blocks, w_ref, up_ref, down_ref,
+           tor_tx, tor_rx, pol_tx, pol_rx, mine_ref, back_ref, member_sums, leader_sums,
+           load_sem, tor_send, tor_recv, pol_send, pol_recv,
+           member_send, member_recv, leader_send, leader_recv, back_send, back_recv):
     tors, pols = sizes
+    halves = 2
+    width = tors // halves
+    columns = pols // GROUP
+    members = halves * GROUP
+    leaders = width * columns
     tor = lax.axis_index("tor")
     pol = lax.axis_index("pol")
     tor_next, tor_prev = lax.rem(tor + 1, tors), lax.rem(tor + tors - 1, tors)
     pol_next, pol_prev = lax.rem(pol + 1, pols), lax.rem(pol + pols - 1, pols)
-    outer, inner = pol // GROUP, lax.rem(pol, GROUP)
-
-    def in_group(stage, rank):
-        if stage == 0:
-            return {"tor": rank, "pol": pol}
-        if stage == 1:
-            return {"tor": tor, "pol": outer * GROUP + rank}
-        return {"tor": tor, "pol": rank * GROUP + inner}
-
-    ranks = [tor, inner, outer]
-    counts = [tors, GROUP, pols // GROUP]
-
-    barrier = pltpu.get_barrier_semaphore()
-    greeted = 0
-    for stage in range(3):
-        for step in range(1, counts[stage]):
-            partner = lax.rem(ranks[stage] + step, counts[stage])
-            pl.semaphore_signal(barrier, inc=1, device_id=in_group(stage, partner), device_id_type=MESH)
-            greeted += 1
-    for neighbour in (pol_next, pol_prev):
-        pl.semaphore_signal(barrier, inc=1, device_id={"tor": tor, "pol": neighbour}, device_id_type=MESH)
-        greeted += 1
+
+    half, lead_tor = tor // width, lax.rem(tor, width)
+    column, inner = pol // GROUP, lax.rem(pol, GROUP)
+    member = half * GROUP + inner
+    leader = lead_tor * columns + column
+    is_leader = member == 1
+    to_leader = {"tor": lead_tor, "pol": column * GROUP + 1}
+
+    def member_at(index):
+        return {"tor": (index // GROUP) * width + lead_tor, "pol": column * GROUP + index % GROUP}
+
+    def leader_at(index):
+        return {"tor": index // columns, "pol": lax.rem(index, columns) * GROUP + 1}
+
+    others = [m for m in range(members) if m != 1]
 
     loads = [
         pltpu.make_async_copy(plasma_hbm, plasma, load_sem.at[0]),
@@ -157,6 +156,20 @@
     for load in loads:
         load.start()
 
+    barrier = pltpu.get_barrier_semaphore()
+    for neighbour in (pol_next, pol_prev):
+        pl.semaphore_signal(barrier, inc=1, device_id={"tor": tor, "pol": neighbour}, device_id_type=MESH)
+    for neighbour in (tor_next, tor_prev):
+        pl.semaphore_signal(barrier, inc=1, device_id={"tor": neighbour, "pol": pol}, device_id_type=MESH)
+
+    @pl.when(is_leader)
+    def _():
+        for index in others:
+            pl.semaphore_signal(barrier, inc=1, device_id=member_at(index), device_id_type=MESH)
+        for step in range(1, leaders):
+            partner = leader_at(lax.rem(leader + step, leaders))
+            pl.semaphore_signal(barrier, inc=1, device_id=partner, device_id_type=MESH)
+
     lane = lax.broadcasted_iota(jnp.int32, (8, 256), 1)
     sub = lax.broadcasted_iota(jnp.int32, (8, 256), 0)
 
@@ -214,25 +227,25 @@
             planes += [both[0:8], both[8:16]]
         return planes
 
-    def precondition(vector):
+    loads[0].wait()
+    pack(3, [plasma[c] for c in range(6)])
+    loads[1].wait()
+    for c in range(6):
+        w_ref[0, c] = right[c]
+
+    def precondition(k):
+        vector = [w_ref[k, c] for c in range(6)]
         result = []
         for a in range(6):
+            if k == 0:
+                loads[3 + a].wait()
             total = blocks[6 * a] * vector[0]
             for b in range(1, 6):
                 total = total + blocks[6 * a + b] * vector[b]
             result.append(total)
         return result
 
-    loads[0].wait()
-    pack(3, [plasma[c] for c in range(6)])
-    pl.semaphore_wait(barrier, greeted)
-    flying = tor_copies(3) + pol_copies(3)
-    for copy in flying:
-        copy.start()
-    for load in loads[1:]:
-        load.wait()
-    eta = resist[...]
-
+    flying = []
     gram_rows = {}
 
     def product(i, j):
@@ -243,18 +256,33 @@
         total = total[:, 0:128] + total[:, 128:256]
         gram_rows[(i, j)] = jnp.sum(total, axis=0, keepdims=True)
 
-    for c in range(6):
-        w_ref[0, c] = right[c]
-
     for k in range(ITERS):
-        t = precondition([w_ref[k, c] for c in range(6)])
-        for c in range(6):
-            t_ref[k, c] = t[c]
+        t = precondition(k)
         pack(k, t)
         tor_moves, pol_moves = tor_copies(k), pol_copies(k)
+        if k == 0:
+
+            @pl.when(is_leader)
+            def _():
+                pl.semaphore_wait(barrier, 4 + leaders - 1)
+
+            @pl.when(jnp.logical_not(is_leader))
+            def _():
+                pl.semaphore_wait(barrier, 4 + 1)
+
         for copy in pol_moves + tor_moves:
             copy.start()
+        if k == 0:
+            state_moves = pol_copies(3) + tor_copies(3)
+            for copy in state_moves:
+                copy.start()
+            flying += state_moves
         flying += pol_moves + tor_moves
+        for c in range(6):
+            t_ref[k, c] = t[c]
+        if k == 0:
+            loads[2].wait()
+        eta = resist[...]
         p = [plasma[c] for c in range(6)]
         f = flux(p, t, 2)
         partial = []
@@ -262,13 +290,13 @@
             coefficient = eta if c < 3 else viscosity
             total = inverse_step * t[c] + coefficient * (6.0 * t[c] - up_depth(t[c]) - down_depth(t[c]))
             if f[c] is not None:
-                half = 0.5 * f[c]
-                total = total + (up_depth(half) - down_depth(half))
+                half_flux = 0.5 * f[c]
+                total = total + (up_depth(half_flux) - down_depth(half_flux))
             partial.append(total)
         for i in range(k + 1):
             product(i, k)
         if k == 0:
-            for copy in flying[0:4]:
+            for copy in state_moves:
                 copy.wait_recv()
             for c in range(6):
                 up_ref[c] = up_row(plasma[c], pol_rx[3, 1, c : c + 1, :])
@@ -309,30 +337,76 @@
     rows = jnp.broadcast_to(jnp.sum(rows, axis=1, keepdims=True), (16, 128))
     mine = jnp.sum(jnp.where(wide_lane == wide_sub, rows, 0.0), axis=0, keepdims=True)
 
-    for stage in range(3):
-        sums[stage, ranks[stage]] = mine
-        moves = []
-        for step in range(1, counts[stage]):
-            partner = lax.rem(ranks[stage] + step, counts[stage])
-            moves.append(
-                pltpu.make_async_remote_copy(
-                    src_ref=sums.at[stage, ranks[stage]],
-                    dst_ref=sums.at[stage, ranks[stage]],
-                    send_sem=sum_send.at[stage, step],
-                    recv_sem=sum_recv.at[stage, step],
-                    device_id=in_group(stage, partner),
-                    device_id_type=MESH,
-                )
+    def tree(values):
+        while len(values) > 1:
+            values = [a + b for a, b in zip(values[0::2], values[1::2])]
+        return values[0]
+
+    def to_member(index):
+        return pltpu.make_async_remote_copy(
+            src_ref=mine_ref,
+            dst_ref=back_ref,
+            send_sem=back_send.at[index],
+            recv_sem=back_recv,
+            device_id=member_at(index),
+            device_id_type=MESH,
+        )
+
+    def member_copy(index):
+        return pltpu.make_async_remote_copy(
+            src_ref=mine_ref,
+            dst_ref=member_sums.at[index],
+            send_sem=member_send,
+            recv_sem=member_recv.at[index],
+            device_id=to_leader,
+            device_id_type=MESH,
+        )
+
+    @pl.when(jnp.logical_not(is_leader))
+    def _():
+        mine_ref[...] = mine
+        upward = member_copy(member)
+        upward.start()
+        upward.wait_send()
+        to_member(0).wait_recv()
+        total_ref[...] = back_ref[...]
+
+    @pl.when(is_leader)
+    def _():
+        member_sums[1] = mine
+        for index in others:
+            member_copy(index).wait_recv()
+        leader_sums[leader] = tree([member_sums[m] for m in range(members)])
+        moves = [
+            pltpu.make_async_remote_copy(
+                src_ref=leader_sums.at[leader],
+                dst_ref=leader_sums.at[leader],
+                send_sem=leader_send.at[step],
+                recv_sem=leader_recv.at[step],
+                device_id=leader_at(lax.rem(leader + step, leaders)),
+                device_id_type=MESH,
             )
+            for step in range(1, leaders)
+        ]
         for copy in moves:
             copy.start()
-        flying += moves
         for copy in moves:
             copy.wait_recv()
-        mine = sums[stage, 0]
-        for rank in range(1, counts[stage]):
-            mine = mine + sums[stage, rank]
-
+        total = tree([leader_sums[m] for m in range(leaders)])
+        mine_ref[...] = total
+        backs = [to_member(index) for index in others]
+        for copy in backs:
+            copy.start()
+        total_ref[...] = total
+        for copy in moves + backs:
+            copy.wait_send()
+
+    for copy in flying:
+        copy.wait_send()
+
+
+def combine(cell_count, t_ref, total_ref, update_ref, est_ref):
+    mine = total_ref[...]
     row_lane = lax.broadcasted_iota(jnp.int32, (1, 128), 1)
     gram = [[None] * (ITERS + 1) for _ in range(ITERS + 1)]
     for index, (i, j) in enumerate(PAIRS):
@@ -345,12 +419,10 @@
     est = jnp.zeros((1, 128), F32)
     for index in range(ITERS):
         est = jnp.where(row_lane == index, estimates[index] * scale, est)
-    est_ref[...] = est
+    est_ref[...] = est[0, 0:ITERS]
     full = [jnp.broadcast_to(jnp.concatenate([a, a], axis=1), (8, 256)) for a in alphas]
     for c in range(6):
         update_ref[c] = full[0] * t_ref[0, c] + full[1] * t_ref[1, c] + full[2] * t_ref[2, c]
-    for copy in flying:
-        copy.wait_send()
 
 
 def solution(mesh):
@@ -360,9 +432,9 @@
         cell_count = plasma_state.size * sizes[0] * sizes[1]
         hbm = pl.BlockSpec(memory_space=pl.ANY)
         vmem = pl.BlockSpec(memory_space=pltpu.VMEM)
-        update, est = pl.pallas_call(
-            functools.partial(kernel, sizes, cell_count),
-            out_shape=(jax.ShapeDtypeStruct((6, 8, 256), F32), jax.ShapeDtypeStruct((1, 128), F32)),
+        tangents, total = pl.pallas_call(
+            functools.partial(kernel, sizes),
+            out_shape=(pltpu.VMEM((ITERS, 6, 8, 256), F32), pltpu.VMEM((1, 128), F32)),
             in_specs=[hbm] * 4,
             out_specs=(vmem, vmem),
             scratch_shapes=[
@@ -371,31 +443,47 @@
                 pltpu.VMEM((8, 256), F32),
                 pltpu.VMEM((36, 8, 256), F32),
                 pltpu.VMEM((ITERS + 1, 6, 8, 256), F32),
-                pltpu.VMEM((ITERS, 6, 8, 256), F32),
                 pltpu.VMEM((6, 8, 256), F32),
                 pltpu.VMEM((6, 8, 256), F32),
                 pltpu.VMEM((4, 48, 256), BF16),
                 pltpu.VMEM((4, 2, 48, 256), BF16),
                 pltpu.VMEM((4, 2, 6, 256), F32),
                 pltpu.VMEM((4, 2, 6, 256), F32),
-                pltpu.VMEM((3, GROUP, 1, 128), F32),
+                pltpu.VMEM((1, 128), F32),
+                pltpu.VMEM((1, 128), F32),
+                pltpu.VMEM((16, 1, 128), F32),
+                pltpu.VMEM((32, 1, 128), F32),
                 pltpu.SemaphoreType.DMA((9,)),
                 pltpu.SemaphoreType.DMA((4, 2)),
                 pltpu.SemaphoreType.DMA((4, 2)),
                 pltpu.SemaphoreType.DMA((4, 2)),
                 pltpu.SemaphoreType.DMA((4, 2)),
-                pltpu.SemaphoreType.DMA((3, GROUP)),
-                pltpu.SemaphoreType.DMA((3, GROUP)),
+                pltpu.SemaphoreType.DMA,
+                pltpu.SemaphoreType.DMA((16,)),
+                pltpu.SemaphoreType.DMA((32,)),
+                pltpu.SemaphoreType.DMA((32,)),
+                pltpu.SemaphoreType.DMA((16,)),
+                pltpu.SemaphoreType.DMA,
             ],
             compiler_params=pltpu.CompilerParams(collective_id=0, has_side_effects=True),
-            name="gmres",
+            name="krylov",
         )(
             plasma_state.reshape(6, 8, 256),
             right_side.reshape(6, 8, 256),
             resistivity.reshape(8, 256),
             jacobi_blocks.reshape(36, 8, 256),
         )
-        return update.reshape(6, 1, 8, 256), est[0, :ITERS]
+        update, est = pl.pallas_call(
+            functools.partial(combine, cell_count),
+            out_shape=(jax.ShapeDtypeStruct((6, 8, 256), F32), jax.ShapeDtypeStruct((ITERS,), F32)),
+            in_specs=[vmem] * 2,
+            out_specs=(vmem, vmem),
+            name="combine",
+        )(
+            pltpu.with_memory_space_constraint(tangents, pltpu.VMEM),
+            pltpu.with_memory_space_constraint(total, pltpu.VMEM),
+        )
+        return update.reshape(6, 1, 8, 256), est
 
     return jax.shard_map(
         shards,

time: 44.3 us -> 39.4 us (0.89)
  local copies, waits for them, and re-layouts: 2.53 us -> 0 us
  Pallas kernels: 40.9 us -> 38.6 us
    pallas_call x1 -> x2, Pallas kernels: 40.9 us -> 38.6 us  [the longest x1 37.7 us: shards(): pl.pallas_call(functools.partial(kernel, sizes), out_shape=(pltpu.VMEM((I...]
    unnamed x3 -> x0, local copies, waits for them, and re-layouts: 2.02 us -> none
    squeeze x1 -> x0, local copies, waits for them, and re-layouts: 0.51 us -> none  [shards(): return (update.reshape(6, 1, 8, 256), est[0, :ITERS])]
where the time goes in v2:
time: 39.4 us; the launch traced here: 39.2 us
  Pallas kernels  38.6 us (98%)
  between operations  0.64 us (2%)
    pallas_call x1, Pallas kernels, shards(): pl.pallas_call(functools.partial(kernel, sizes), out_shape=(pltpu.VMEM((I...  37.7 us
    pallas_call x1, Pallas kernels, shards(): pl.pallas_call(functools.partial(combine, cell_count), out_shape=(jax.Sha...  0.84 us

profile of v2, /device:TPU:1, one launch (start us, length us, event | category | flops | bytes accessed | tf_op | source)
XLA Modules:
  0.0 39.2 jit_solution(14851665151142803912)
XLA Ops:
  0.6 37.7 %krylov.1 = (f32[3,6,8,256]{3,2,1,0:T(8,128)S(1)}, f32[1,128]{1,0:T(1,128)S(1)}) custom-call(f32[6,8,256]{2,1,0:T(8,128)} %bitcast.8, f32[6,8,256]{2,1,0:T(8,128)} %bitcast.9, f32[8,256]{1,0:T(8,128)} %bitcast.10, f32[36,8,256]{2,1,0:T(8,128)} %bitcast.7), custom_call_target="tpu_custom_call" | custom-call | tf_op jit(solution)/shard_map/krylov/pallas_call | solution.py:435
  38.4 0.8 %combine.1 = (f32[6,8,256]{2,1,0:T(8,128)}, f32[3]{0:T(128)}) custom-call(f32[3,6,8,256]{3,2,1,0:T(8,128)S(1)} %get-tuple-element.6.t_ref, f32[1,128]{1,0:T(1,128)S(1)} %get-tuple-element.7.total_ref), custom_call_target="tpu_custom_call" | custom-call | tf_op jit(solution)/shard_map/combine/pallas_call | solution.py:476

commit v3 on v2

--- a/solution.py
+++ b/solution.py
@@ -111,11 +111,11 @@
     return alphas, estimates
 
 
-def kernel(sizes, plasma_hbm, right_hbm, resist_hbm, blocks_hbm, t_ref, total_ref,
+def kernel(sizes, scale, plasma_hbm, right_hbm, resist_hbm, blocks_hbm, t_ref, weights_ref,
            plasma, right, resist, blocks, w_ref, up_ref, down_ref,
-           tor_tx, tor_rx, pol_tx, pol_rx, mine_ref, back_ref, member_sums, leader_sums,
+           tor_tx, tor_rx, pol_tx, pol_rx, mine_ref, back_ref, sum_ref, all_sums,
            load_sem, tor_send, tor_recv, pol_send, pol_recv,
-           member_send, member_recv, leader_send, leader_recv, back_send, back_recv):
+           root_send, root_recv, back_send, back_recv):
     tors, pols = sizes
     halves = 2
     width = tors // halves
@@ -141,6 +141,12 @@
         return {"tor": index // columns, "pol": lax.rem(index, columns) * GROUP + 1}
 
     others = [m for m in range(members) if m != 1]
+
+    barrier = pltpu.get_barrier_semaphore()
+    for neighbour in (pol_next, pol_prev):
+        pl.semaphore_signal(barrier, inc=1, device_id={"tor": tor, "pol": neighbour}, device_id_type=MESH)
+    for neighbour in (tor_next, tor_prev):
+        pl.semaphore_signal(barrier, inc=1, device_id={"tor": neighbour, "pol": pol}, device_id_type=MESH)
 
     loads = [
         pltpu.make_async_copy(plasma_hbm, plasma, load_sem.at[0]),
@@ -156,19 +162,14 @@
     for load in loads:
         load.start()
 
-    barrier = pltpu.get_barrier_semaphore()
-    for neighbour in (pol_next, pol_prev):
-        pl.semaphore_signal(barrier, inc=1, device_id={"tor": tor, "pol": neighbour}, device_id_type=MESH)
-    for neighbour in (tor_next, tor_prev):
-        pl.semaphore_signal(barrier, inc=1, device_id={"tor": neighbour, "pol": pol}, device_id_type=MESH)
-
     @pl.when(is_leader)
     def _():
-        for index in others:
-            pl.semaphore_signal(barrier, inc=1, device_id=member_at(index), device_id_type=MESH)
         for step in range(1, leaders):
             partner = leader_at(lax.rem(leader + step, leaders))
             pl.semaphore_signal(barrier, inc=1, device_id=partner, device_id_type=MESH)
+        pl.semaphore_wait(barrier, 4 + leaders - 1)
+        for index in others:
+            pl.semaphore_signal(barrier, inc=1, device_id=member_at(index), device_id_type=MESH)
 
     lane = lax.broadcasted_iota(jnp.int32, (8, 256), 1)
     sub = lax.broadcasted_iota(jnp.int32, (8, 256), 0)
@@ -261,10 +262,6 @@
         pack(k, t)
         tor_moves, pol_moves = tor_copies(k), pol_copies(k)
         if k == 0:
-
-            @pl.when(is_leader)
-            def _():
-                pl.semaphore_wait(barrier, 4 + leaders - 1)
 
             @pl.when(jnp.logical_not(is_leader))
             def _():
@@ -344,7 +341,7 @@
 
     def to_member(index):
         return pltpu.make_async_remote_copy(
-            src_ref=mine_ref,
+            src_ref=sum_ref,
             dst_ref=back_ref,
             send_sem=back_send.at[index],
             recv_sem=back_recv,
@@ -352,75 +349,86 @@
             device_id_type=MESH,
         )
 
-    def member_copy(index):
+    place = leader * members + member
+    slot = (place // 8, pl.ds(lax.rem(place, 8), 1))
+
+    def to_root(index):
         return pltpu.make_async_remote_copy(
             src_ref=mine_ref,
-            dst_ref=member_sums.at[index],
-            send_sem=member_send,
-            recv_sem=member_recv.at[index],
-            device_id=to_leader,
+            dst_ref=all_sums.at[slot[0], slot[1]],
+            send_sem=root_send.at[index],
+            recv_sem=root_recv,
+            device_id={"tor": index // columns, "pol": (index % columns) * GROUP + 1},
             device_id_type=MESH,
         )
 
+    own = pltpu.make_async_copy(mine_ref, all_sums.at[slot[0], slot[1]], root_recv)
+    order = sorted(range(leaders), key=lambda r: r // columns + r % columns)
+
+    def solve(total):
+        row_lane = lax.broadcasted_iota(jnp.int32, (1, 128), 1)
+        gram = [[None] * (ITERS + 1) for _ in range(ITERS + 1)]
+        for index, (i, j) in enumerate(PAIRS):
+            entry = jnp.sum(jnp.where(row_lane == index, total, 0.0), axis=1, keepdims=True)
+            entry = jnp.broadcast_to(entry, (1, 128))
+            gram[i][j] = entry
+            gram[j][i] = entry
+        alphas, estimates = small_solve(gram, gram[0][0])
+        est = jnp.zeros((1, 128), F32)
+        for index in range(ITERS):
+            est = jnp.where(row_lane == index, estimates[index] * scale, est)
+        for index in range(ITERS):
+            weights_ref[index : index + 1, :] = alphas[index]
+        weights_ref[ITERS : ITERS + 1, :] = est
+
+    mine_ref[...] = mine
+
     @pl.when(jnp.logical_not(is_leader))
     def _():
-        mine_ref[...] = mine
-        upward = member_copy(member)
-        upward.start()
-        upward.wait_send()
+        for index in order:
+            to_root(index).start()
+        for copy in flying:
+            copy.wait_send()
+        for index in order:
+            to_root(index).wait_send()
         to_member(0).wait_recv()
-        total_ref[...] = back_ref[...]
+        solve(back_ref[...])
 
     @pl.when(is_leader)
     def _():
-        member_sums[1] = mine
-        for index in others:
-            member_copy(index).wait_recv()
-        leader_sums[leader] = tree([member_sums[m] for m in range(members)])
-        moves = [
-            pltpu.make_async_remote_copy(
-                src_ref=leader_sums.at[leader],
-                dst_ref=leader_sums.at[leader],
-                send_sem=leader_send.at[step],
-                recv_sem=leader_recv.at[step],
-                device_id=leader_at(lax.rem(leader + step, leaders)),
-                device_id_type=MESH,
-            )
-            for step in range(1, leaders)
-        ]
-        for copy in moves:
-            copy.start()
-        for copy in moves:
-            copy.wait_recv()
-        total = tree([leader_sums[m] for m in range(leaders)])
-        mine_ref[...] = total
+        own.start()
+        for index in order:
+
+            @pl.when(leader != index)
+            def _():
+                to_root(index).start()
+
+        for copy in flying:
+            copy.wait_send()
+        for index in order:
+
+            @pl.when(leader != index)
+            def _():
+                to_root(index).wait_send()
+
+        pltpu.make_async_copy(all_sums, all_sums, root_recv).wait()
+        total = tree([all_sums[m] for m in range(tors * pols // 8)])
+        total = jnp.sum(total, axis=0, keepdims=True)
+        sum_ref[...] = total
         backs = [to_member(index) for index in others]
         for copy in backs:
             copy.start()
-        total_ref[...] = total
-        for copy in moves + backs:
+        solve(total)
+        for copy in backs:
             copy.wait_send()
 
-    for copy in flying:
-        copy.wait_send()
-
-
-def combine(cell_count, t_ref, total_ref, update_ref, est_ref):
-    mine = total_ref[...]
-    row_lane = lax.broadcasted_iota(jnp.int32, (1, 128), 1)
-    gram = [[None] * (ITERS + 1) for _ in range(ITERS + 1)]
-    for index, (i, j) in enumerate(PAIRS):
-        entry = jnp.sum(jnp.where(row_lane == index, mine, 0.0), axis=1, keepdims=True)
-        entry = jnp.broadcast_to(entry, (1, 128))
-        gram[i][j] = entry
-        gram[j][i] = entry
-    alphas, estimates = small_solve(gram, gram[0][0])
-    scale = 1.0 / float(cell_count) ** 0.5
-    est = jnp.zeros((1, 128), F32)
-    for index in range(ITERS):
-        est = jnp.where(row_lane == index, estimates[index] * scale, est)
-    est_ref[...] = est[0, 0:ITERS]
-    full = [jnp.broadcast_to(jnp.concatenate([a, a], axis=1), (8, 256)) for a in alphas]
+
+def combine(t_ref, weights_ref, update_ref, est_ref):
+    est_ref[...] = weights_ref[ITERS, 0:ITERS]
+    full = []
+    for k in range(ITERS):
+        alpha = weights_ref[k : k + 1, :]
+        full.append(jnp.broadcast_to(jnp.concatenate([alpha, alpha], axis=1), (8, 256)))
     for c in range(6):
         update_ref[c] = full[0] * t_ref[0, c] + full[1] * t_ref[1, c] + full[2] * t_ref[2, c]
 
@@ -429,12 +437,12 @@
     sizes = (mesh.shape["tor"], mesh.shape["pol"])
 
     def shards(plasma_state, right_side, resistivity, jacobi_blocks):
-        cell_count = plasma_state.size * sizes[0] * sizes[1]
+        scale = 1.0 / float(plasma_state.size * sizes[0] * sizes[1]) ** 0.5
         hbm = pl.BlockSpec(memory_space=pl.ANY)
         vmem = pl.BlockSpec(memory_space=pltpu.VMEM)
-        tangents, total = pl.pallas_call(
-            functools.partial(kernel, sizes),
-            out_shape=(pltpu.VMEM((ITERS, 6, 8, 256), F32), pltpu.VMEM((1, 128), F32)),
+        tangents, weights = pl.pallas_call(
+            functools.partial(kernel, sizes, scale),
+            out_shape=(pltpu.VMEM((ITERS, 6, 8, 256), F32), pltpu.VMEM((ITERS + 1, 128), F32)),
             in_specs=[hbm] * 4,
             out_specs=(vmem, vmem),
             scratch_shapes=[
@@ -451,17 +459,15 @@
                 pltpu.VMEM((4, 2, 6, 256), F32),
                 pltpu.VMEM((1, 128), F32),
                 pltpu.VMEM((1, 128), F32),
-                pltpu.VMEM((16, 1, 128), F32),
-                pltpu.VMEM((32, 1, 128), F32),
+                pltpu.VMEM((1, 128), F32),
+                pltpu.VMEM((64, 8, 128), F32),
                 pltpu.SemaphoreType.DMA((9,)),
                 pltpu.SemaphoreType.DMA((4, 2)),
                 pltpu.SemaphoreType.DMA((4, 2)),
                 pltpu.SemaphoreType.DMA((4, 2)),
                 pltpu.SemaphoreType.DMA((4, 2)),
+                pltpu.SemaphoreType.DMA((32,)),
                 pltpu.SemaphoreType.DMA,
-                pltpu.SemaphoreType.DMA((16,)),
-                pltpu.SemaphoreType.DMA((32,)),
-                pltpu.SemaphoreType.DMA((32,)),
                 pltpu.SemaphoreType.DMA((16,)),
                 pltpu.SemaphoreType.DMA,
             ],
@@ -474,14 +480,14 @@
             jacobi_blocks.reshape(36, 8, 256),
         )
         update, est = pl.pallas_call(
-            functools.partial(combine, cell_count),
+            combine,
             out_shape=(jax.ShapeDtypeStruct((6, 8, 256), F32), jax.ShapeDtypeStruct((ITERS,), F32)),
             in_specs=[vmem] * 2,
             out_specs=(vmem, vmem),
             name="combine",
         )(
             pltpu.with_memory_space_constraint(tangents, pltpu.VMEM),
-            pltpu.with_memory_space_constraint(total, pltpu.VMEM),
+            pltpu.with_memory_space_constraint(weights, pltpu.VMEM),
         )
         return update.reshape(6, 1, 8, 256), est
 

time: 39.4 us -> 37.4 us (0.949)
  Pallas kernels: 38.6 us -> 36.6 us
    pallas_call x2, Pallas kernels: 38.6 us -> 36.6 us  [the longest x1 36 us: shards(): pl.pallas_call(functools.partial(kernel, sizes, scale), out_shape=(pltpu....]
where the time goes in v3:
time: 37.4 us; the launch traced here: 37.3 us
  Pallas kernels  36.6 us (98%)
  between operations  0.64 us (2%)
    pallas_call x1, Pallas kernels, shards(): pl.pallas_call(functools.partial(kernel, sizes, scale), out_shape=(pltpu....  36 us

profile of v3, /device:TPU:1, one launch (start us, length us, event | category | flops | bytes accessed | tf_op | source)
XLA Modules:
  0.0 37.3 jit_solution(1876782108655735992)
XLA Ops:
  0.6 36.0 %krylov.1 = (f32[3,6,8,256]{3,2,1,0:T(8,128)S(1)}, f32[4,128]{1,0:T(4,128)S(1)}) custom-call(f32[6,8,256]{2,1,0:T(8,128)} %bitcast.8, f32[6,8,256]{2,1,0:T(8,128)} %bitcast.9, f32[8,256]{1,0:T(8,128)} %bitcast.10, f32[36,8,256]{2,1,0:T(8,128)} %bitcast.7), custom_call_target="tpu_custom_call" | custom-call | tf_op jit(solution)/shard_map/krylov/pallas_call | solution.py:443
  36.6 0.6 %combine.1 = (f32[6,8,256]{2,1,0:T(8,128)}, f32[3]{0:T(128)}) custom-call(f32[3,6,8,256]{3,2,1,0:T(8,128)S(1)} %get-tuple-element.6.t_ref, f32[4,128]{1,0:T(4,128)S(1)} %get-tuple-element.7.weights_ref), custom_call_target="tpu_custom_call" | custom-call | tf_op jit(solution)/shard_map/combine/pallas_call | solution.py:482

commit v4 on v3

--- a/solution.py
+++ b/solution.py
@@ -131,16 +131,27 @@
     column, inner = pol // GROUP, lax.rem(pol, GROUP)
     member = half * GROUP + inner
     leader = lead_tor * columns + column
-    is_leader = member == 1
-    to_leader = {"tor": lead_tor, "pol": column * GROUP + 1}
+    roots = leaders + 1
+    root = tor * columns + column
+    is_root = jnp.logical_and(inner == 1, root < roots)
 
     def member_at(index):
         return {"tor": (index // GROUP) * width + lead_tor, "pol": column * GROUP + index % GROUP}
 
-    def leader_at(index):
+    def root_at(index):
         return {"tor": index // columns, "pol": lax.rem(index, columns) * GROUP + 1}
 
-    others = [m for m in range(members) if m != 1]
+    def for_members(act):
+        @pl.when(root != 0)
+        def _():
+            for index in range(members):
+                if index not in (1, GROUP + 1):
+                    act(index)
+
+        @pl.when(jnp.logical_and(root != 0, root != leaders))
+        def _():
+            act(GROUP + 1)
+
 
     barrier = pltpu.get_barrier_semaphore()
     for neighbour in (pol_next, pol_prev):
@@ -162,14 +173,15 @@
     for load in loads:
         load.start()
 
-    @pl.when(is_leader)
+    @pl.when(is_root)
     def _():
-        for step in range(1, leaders):
-            partner = leader_at(lax.rem(leader + step, leaders))
+        for step in range(1, roots):
+            partner = root_at(lax.rem(root + step, roots))
             pl.semaphore_signal(barrier, inc=1, device_id=partner, device_id_type=MESH)
-        pl.semaphore_wait(barrier, 4 + leaders - 1)
-        for index in others:
-            pl.semaphore_signal(barrier, inc=1, device_id=member_at(index), device_id_type=MESH)
+        pl.semaphore_wait(barrier, 4 + roots - 1)
+        for_members(
+            lambda index: pl.semaphore_signal(barrier, inc=1, device_id=member_at(index), device_id_type=MESH)
+        )
 
     lane = lax.broadcasted_iota(jnp.int32, (8, 256), 1)
     sub = lax.broadcasted_iota(jnp.int32, (8, 256), 0)
@@ -212,14 +224,16 @@
             for way in range(2)
         ]
 
-    def pack(slot, x):
-        for c in range(6):
-            pol_tx[slot, 0, c : c + 1, :] = x[c][7:8, :]
-            pol_tx[slot, 1, c : c + 1, :] = x[c][0:1, :]
+    def pack_tor(slot, x):
         for pair in range(3):
             tor_tx[slot, 16 * pair : 16 * pair + 16, :] = jnp.concatenate(
                 [x[2 * pair], x[2 * pair + 1]], axis=0
             ).astype(BF16)
+
+    def pack_pol(slot, x):
+        for c in range(6):
+            pol_tx[slot, 0, c : c + 1, :] = x[c][7:8, :]
+            pol_tx[slot, 1, c : c + 1, :] = x[c][0:1, :]
 
     def from_tor(slot, way):
         planes = []
@@ -229,7 +243,8 @@
         return planes
 
     loads[0].wait()
-    pack(3, [plasma[c] for c in range(6)])
+    pack_tor(3, [plasma[c] for c in range(6)])
+    pack_pol(3, [plasma[c] for c in range(6)])
     loads[1].wait()
     for c in range(6):
         w_ref[0, c] = right[c]
@@ -259,18 +274,21 @@
 
     for k in range(ITERS):
         t = precondition(k)
-        pack(k, t)
+        pack_tor(k, t)
         tor_moves, pol_moves = tor_copies(k), pol_copies(k)
         if k == 0:
 
-            @pl.when(jnp.logical_not(is_leader))
+            @pl.when(jnp.logical_not(is_root))
             def _():
                 pl.semaphore_wait(barrier, 4 + 1)
 
-        for copy in pol_moves + tor_moves:
+        for copy in tor_moves:
+            copy.start()
+        pack_pol(k, t)
+        for copy in pol_moves:
             copy.start()
         if k == 0:
-            state_moves = pol_copies(3) + tor_copies(3)
+            state_moves = tor_copies(3) + pol_copies(3)
             for copy in state_moves:
                 copy.start()
             flying += state_moves
@@ -363,7 +381,7 @@
         )
 
     own = pltpu.make_async_copy(mine_ref, all_sums.at[slot[0], slot[1]], root_recv)
-    order = sorted(range(leaders), key=lambda r: r // columns + r % columns)
+    order = sorted(range(roots), key=lambda r: r // columns + r % columns)
 
     def solve(total):
         row_lane = lax.broadcasted_iota(jnp.int32, (1, 128), 1)
@@ -383,7 +401,7 @@
 
     mine_ref[...] = mine
 
-    @pl.when(jnp.logical_not(is_leader))
+    @pl.when(jnp.logical_not(is_root))
     def _():
         for index in order:
             to_root(index).start()
@@ -394,12 +412,12 @@
         to_member(0).wait_recv()
         solve(back_ref[...])
 
-    @pl.when(is_leader)
+    @pl.when(is_root)
     def _():
         own.start()
         for index in order:
 
-            @pl.when(leader != index)
+            @pl.when(root != index)
             def _():
                 to_root(index).start()
 
@@ -407,7 +425,7 @@
             copy.wait_send()
         for index in order:
 
-            @pl.when(leader != index)
+            @pl.when(root != index)
             def _():
                 to_root(index).wait_send()
 
@@ -415,12 +433,9 @@
         total = tree([all_sums[m] for m in range(tors * pols // 8)])
         total = jnp.sum(total, axis=0, keepdims=True)
         sum_ref[...] = total
-        backs = [to_member(index) for index in others]
-        for copy in backs:
-            copy.start()
+        for_members(lambda index: to_member(index).start())
         solve(total)
-        for copy in backs:
-            copy.wait_send()
+        for_members(lambda index: to_member(index).wait_send())
 
 
 def combine(t_ref, weights_ref, update_ref, est_ref):
@@ -466,7 +481,7 @@
                 pltpu.SemaphoreType.DMA((4, 2)),
                 pltpu.SemaphoreType.DMA((4, 2)),
                 pltpu.SemaphoreType.DMA((4, 2)),
-                pltpu.SemaphoreType.DMA((32,)),
+                pltpu.SemaphoreType.DMA((33,)),
                 pltpu.SemaphoreType.DMA,
                 pltpu.SemaphoreType.DMA((16,)),
                 pltpu.SemaphoreType.DMA,

time: 37.4 us -> 36.6 us (0.979)
  Pallas kernels: 36.6 us -> 35.8 us
    pallas_call x1, Pallas kernels: 36 us -> 35.2 us  [shards(): pl.pallas_call(functools.partial(kernel, sizes, scale), out_shape=(pltpu....]
where the time goes in v4:
time: 36.6 us; the launch traced here: 36.5 us
  Pallas kernels  35.8 us (98%)
  between operations  0.64 us (2%)
    pallas_call x1, Pallas kernels, shards(): pl.pallas_call(functools.partial(kernel, sizes, scale), out_shape=(pltpu....  35.2 us

profile of v4, /device:TPU:1, one launch (start us, length us, event | category | flops | bytes accessed | tf_op | source)
XLA Modules:
  0.0 36.5 jit_solution(3162286270471353852)
XLA Ops:
  0.6 35.2 %krylov.1 = (f32[3,6,8,256]{3,2,1,0:T(8,128)S(1)}, f32[4,128]{1,0:T(4,128)S(1)}) custom-call(f32[6,8,256]{2,1,0:T(8,128)} %bitcast.8, f32[6,8,256]{2,1,0:T(8,128)} %bitcast.9, f32[8,256]{1,0:T(8,128)} %bitcast.10, f32[36,8,256]{2,1,0:T(8,128)} %bitcast.7), custom_call_target="tpu_custom_call" | custom-call | tf_op jit(solution)/shard_map/krylov/pallas_call | solution.py:458
  35.8 0.6 %combine.1 = (f32[6,8,256]{2,1,0:T(8,128)}, f32[3]{0:T(128)}) custom-call(f32[3,6,8,256]{3,2,1,0:T(8,128)S(1)} %get-tuple-element.6.t_ref, f32[4,128]{1,0:T(4,128)S(1)} %get-tuple-element.7.weights_ref), custom_call_target="tpu_custom_call" | custom-call | tf_op jit(solution)/shard_map/combine/pallas_call | solution.py:497

commit v5 on v4

--- a/solution.py
+++ b/solution.py
@@ -113,7 +113,7 @@
 
 def kernel(sizes, scale, plasma_hbm, right_hbm, resist_hbm, blocks_hbm, t_ref, weights_ref,
            plasma, right, resist, blocks, w_ref, up_ref, down_ref,
-           tor_tx, tor_rx, pol_tx, pol_rx, mine_ref, back_ref, sum_ref, all_sums,
+           tor_tx, tor_rx, pol_tx, pol_rx, mix_tx, mix_rx, edge_tx, edge_rx, mine_ref, back_ref, sum_ref, all_sums,
            load_sem, tor_send, tor_recv, pol_send, pol_recv,
            root_send, root_recv, back_send, back_recv):
     tors, pols = sizes
@@ -154,10 +154,10 @@
 
 
     barrier = pltpu.get_barrier_semaphore()
+    for neighbour in (tor_next, tor_prev):
+        pl.semaphore_signal(barrier, inc=1, device_id={"tor": neighbour, "pol": pol}, device_id_type=MESH)
     for neighbour in (pol_next, pol_prev):
         pl.semaphore_signal(barrier, inc=1, device_id={"tor": tor, "pol": neighbour}, device_id_type=MESH)
-    for neighbour in (tor_next, tor_prev):
-        pl.semaphore_signal(barrier, inc=1, device_id={"tor": neighbour, "pol": pol}, device_id_type=MESH)
 
     loads = [
         pltpu.make_async_copy(plasma_hbm, plasma, load_sem.at[0]),
@@ -224,6 +224,49 @@
             for way in range(2)
         ]
 
+    def mixed(t, direction):
+        f = flux(own_plasma, t, direction)
+        half = [None if f[c] is None else 0.5 * f[c] for c in range(6)]
+        planes = []
+        for sign in (-1.0, 1.0):
+            planes.append(
+                [sign * half[c] - viscosity * t[c] for c in (3, 4, 5)]
+                + [t[0], t[1], t[2]]
+                + [sign * half[c] for c in range(3) if c != direction]
+            )
+        return planes
+
+    def mixed_copies(tor_way):
+        if tor_way:
+            src, dst, send, recv = mix_tx, mix_rx, tor_send, tor_recv
+        else:
+            src, dst, send, recv = edge_tx, edge_rx, pol_send, pol_recv
+        return [
+            pltpu.make_async_remote_copy(
+                src_ref=src.at[way],
+                dst_ref=dst.at[way],
+                send_sem=send.at[0, way],
+                recv_sem=recv.at[0, way],
+                device_id=(
+                    {"tor": (tor_next, tor_prev)[way], "pol": pol}
+                    if tor_way
+                    else {"tor": tor, "pol": (pol_next, pol_prev)[way]}
+                ),
+                device_id_type=MESH,
+            )
+            for way in range(2)
+        ]
+
+    def add_mixed(partial, planes, direction):
+        partial = list(partial)
+        others = [c for c in range(3) if c != direction]
+        for index in range(3):
+            partial[3 + index] = partial[3 + index] + planes[index]
+            partial[index] = partial[index] - eta * planes[3 + index]
+        for index, c in enumerate(others):
+            partial[c] = partial[c] + planes[6 + index]
+        return partial
+
     def pack_tor(slot, x):
         for pair in range(3):
             tor_tx[slot, 16 * pair : 16 * pair + 16, :] = jnp.concatenate(
@@ -243,8 +286,9 @@
         return planes
 
     loads[0].wait()
-    pack_tor(3, [plasma[c] for c in range(6)])
-    pack_pol(3, [plasma[c] for c in range(6)])
+    own_plasma = [plasma[c] for c in range(6)]
+    pack_tor(3, own_plasma)
+    pack_pol(3, own_plasma)
     loads[1].wait()
     for c in range(6):
         w_ref[0, c] = right[c]
@@ -272,34 +316,8 @@
         total = total[:, 0:128] + total[:, 128:256]
         gram_rows[(i, j)] = jnp.sum(total, axis=0, keepdims=True)
 
-    for k in range(ITERS):
-        t = precondition(k)
-        pack_tor(k, t)
-        tor_moves, pol_moves = tor_copies(k), pol_copies(k)
-        if k == 0:
-
-            @pl.when(jnp.logical_not(is_root))
-            def _():
-                pl.semaphore_wait(barrier, 4 + 1)
-
-        for copy in tor_moves:
-            copy.start()
-        pack_pol(k, t)
-        for copy in pol_moves:
-            copy.start()
-        if k == 0:
-            state_moves = tor_copies(3) + pol_copies(3)
-            for copy in state_moves:
-                copy.start()
-            flying += state_moves
-        flying += pol_moves + tor_moves
-        for c in range(6):
-            t_ref[k, c] = t[c]
-        if k == 0:
-            loads[2].wait()
-        eta = resist[...]
-        p = [plasma[c] for c in range(6)]
-        f = flux(p, t, 2)
+    def local(t):
+        f = flux(own_plasma, t, 2)
         partial = []
         for c in range(6):
             coefficient = eta if c < 3 else viscosity
@@ -308,9 +326,69 @@
                 half_flux = 0.5 * f[c]
                 total = total + (up_depth(half_flux) - down_depth(half_flux))
             partial.append(total)
+        return partial
+
+    def outside(way, row):
+        return jnp.where(pol == (pols - 1 if way == 1 else 0), 0.0, row)
+
+    t = precondition(0)
+    along_tor, along_pol = mixed(t, 0), mixed(t, 1)
+    for way in range(2):
+        for pair in range(4):
+            mix_tx[way, 16 * pair : 16 * pair + 16, :] = jnp.concatenate(
+                [along_tor[way][2 * pair], along_tor[way][2 * pair + 1]], axis=0
+            ).astype(BF16)
+        for index in range(8):
+            edge_tx[way, index : index + 1, :] = along_pol[way][index][7 - 7 * way : 8 - 7 * way, :]
+
+    @pl.when(jnp.logical_not(is_root))
+    def _():
+        pl.semaphore_wait(barrier, 4 + 1)
+
+    tor_moves, pol_moves = mixed_copies(True), mixed_copies(False)
+    state_moves = tor_copies(3) + pol_copies(3)
+    for copy in tor_moves + pol_moves + state_moves:
+        copy.start()
+    flying += tor_moves + pol_moves + state_moves
+    for c in range(6):
+        t_ref[0, c] = t[c]
+    loads[2].wait()
+    eta = resist[...]
+    partial = local(t)
+    product(0, 0)
+    for copy in pol_moves:
+        copy.wait_recv()
+    after = [outside(1, edge_rx[1, index : index + 1, :]) for index in range(8)]
+    before = [outside(0, edge_rx[0, index : index + 1, :]) for index in range(8)]
+    partial = add_mixed(partial, [up_row(along_pol[1][index], after[index]) for index in range(8)], 1)
+    partial = add_mixed(partial, [down_row(along_pol[0][index], before[index]) for index in range(8)], 1)
+    for copy in tor_moves:
+        copy.wait_recv()
+    for way in range(2):
+        planes = []
+        for pair in range(4):
+            both = mix_rx[way, 16 * pair : 16 * pair + 16, :].astype(F32)
+            planes += [both[0:8], both[8:16]]
+        partial = add_mixed(partial, planes, 0)
+    for c in range(6):
+        w_ref[1, c] = partial[c]
+
+    for k in range(1, ITERS):
+        t = precondition(k)
+        pack_tor(k, t)
+        tor_moves, pol_moves = tor_copies(k), pol_copies(k)
+        for copy in tor_moves:
+            copy.start()
+        pack_pol(k, t)
+        for copy in pol_moves:
+            copy.start()
+        flying += pol_moves + tor_moves
+        for c in range(6):
+            t_ref[k, c] = t[c]
+        partial = local(t)
         for i in range(k + 1):
             product(i, k)
-        if k == 0:
+        if k == 1:
             for copy in state_moves:
                 copy.wait_recv()
             for c in range(6):
@@ -318,10 +396,8 @@
                 down_ref[c] = down_row(plasma[c], pol_rx[3, 0, c : c + 1, :])
         for copy in pol_moves:
             copy.wait_recv()
-        t_up = [
-            up_row(t[c], jnp.where(pol == pols - 1, 0.0, pol_rx[k, 1, c : c + 1, :])) for c in range(6)
-        ]
-        t_down = [down_row(t[c], jnp.where(pol == 0, 0.0, pol_rx[k, 0, c : c + 1, :])) for c in range(6)]
+        t_up = [up_row(t[c], outside(1, pol_rx[k, 1, c : c + 1, :])) for c in range(6)]
+        t_down = [down_row(t[c], outside(0, pol_rx[k, 0, c : c + 1, :])) for c in range(6)]
         f_up = flux([up_ref[c] for c in range(6)], t_up, 1)
         f_down = flux([down_ref[c] for c in range(6)], t_down, 1)
         for c in range(6):
@@ -472,6 +548,10 @@
                 pltpu.VMEM((4, 2, 48, 256), BF16),
                 pltpu.VMEM((4, 2, 6, 256), F32),
                 pltpu.VMEM((4, 2, 6, 256), F32),
+                pltpu.VMEM((2, 64, 256), BF16),
+                pltpu.VMEM((2, 64, 256), BF16),
+                pltpu.VMEM((2, 8, 256), F32),
+                pltpu.VMEM((2, 8, 256), F32),
                 pltpu.VMEM((1, 128), F32),
                 pltpu.VMEM((1, 128), F32),
                 pltpu.VMEM((1, 128), F32),

time: 36.6 us -> 36.1 us (0.986)
  Pallas kernels: 35.8 us -> 35.3 us
    pallas_call x1, Pallas kernels: 35.2 us -> 34.6 us  [shards(): pl.pallas_call(functools.partial(kernel, sizes, scale), out_shape=(pltpu....]
where the time goes in v5:
time: 36.1 us; the launch traced here: 35.9 us
  Pallas kernels  35.3 us (98%)
  between operations  0.64 us (2%)
    pallas_call x1, Pallas kernels, shards(): pl.pallas_call(functools.partial(kernel, sizes, scale), out_shape=(pltpu....  34.6 us

profile of v5, /device:TPU:1, one launch (start us, length us, event | category | flops | bytes accessed | tf_op | source)
XLA Modules:
  0.0 35.9 jit_solution(13381536292517187587)
XLA Ops:
  0.6 34.6 %krylov.1 = (f32[3,6,8,256]{3,2,1,0:T(8,128)S(1)}, f32[4,128]{1,0:T(4,128)S(1)}) custom-call(f32[6,8,256]{2,1,0:T(8,128)} %bitcast.8, f32[6,8,256]{2,1,0:T(8,128)} %bitcast.9, f32[8,256]{1,0:T(8,128)} %bitcast.10, f32[36,8,256]{2,1,0:T(8,128)} %bitcast.7), custom_call_target="tpu_custom_call" | custom-call | tf_op jit(solution)/shard_map/krylov/pallas_call | solution.py:534
  35.3 0.6 %combine.1 = (f32[6,8,256]{2,1,0:T(8,128)}, f32[3]{0:T(128)}) custom-call(f32[3,6,8,256]{3,2,1,0:T(8,128)S(1)} %get-tuple-element.6.t_ref, f32[4,128]{1,0:T(4,128)S(1)} %get-tuple-element.7.weights_ref), custom_call_target="tpu_custom_call" | custom-call | tf_op jit(solution)/shard_map/combine/pallas_call | solution.py:577

commit v6 on v5

--- a/solution.py
+++ b/solution.py
@@ -113,7 +113,7 @@
 
 def kernel(sizes, scale, plasma_hbm, right_hbm, resist_hbm, blocks_hbm, t_ref, weights_ref,
            plasma, right, resist, blocks, w_ref, up_ref, down_ref,
-           tor_tx, tor_rx, pol_tx, pol_rx, mix_tx, mix_rx, edge_tx, edge_rx, mine_ref, back_ref, sum_ref, all_sums,
+           tor_tx, tor_rx, pol_tx, pol_rx, mix_tx, mix_rx, edge_tx, edge_rx, mine_ref, back_ref, sum_ref, all_sums, size_ref,
            load_sem, tor_send, tor_recv, pol_send, pol_recv,
            root_send, root_recv, back_send, back_recv):
     tors, pols = sizes
@@ -164,12 +164,7 @@
         pltpu.make_async_copy(right_hbm, right, load_sem.at[1]),
         pltpu.make_async_copy(resist_hbm, resist, load_sem.at[2]),
     ]
-    for row in range(6):
-        loads.append(
-            pltpu.make_async_copy(
-                blocks_hbm.at[pl.ds(6 * row, 6)], blocks.at[pl.ds(6 * row, 6)], load_sem.at[3 + row]
-            )
-        )
+    loads.append(pltpu.make_async_copy(blocks_hbm, blocks, load_sem.at[3]))
     for load in loads:
         load.start()
 
@@ -198,13 +193,16 @@
     def down_row(x, halo):
         return jnp.where(sub == 0, jnp.broadcast_to(halo, (8, 256)), pltpu.roll(x, 1, 0))
 
+    def wait_bytes(ref, sem):
+        pltpu.make_async_copy(ref, ref, sem).wait()
+
     def tor_copies(slot):
         return [
             pltpu.make_async_remote_copy(
                 src_ref=tor_tx.at[slot],
                 dst_ref=tor_rx.at[slot, way],
-                send_sem=tor_send.at[slot, way],
-                recv_sem=tor_recv.at[slot, way],
+                send_sem=tor_send.at[0],
+                recv_sem=tor_recv.at[slot],
                 device_id={"tor": (tor_next, tor_prev)[way], "pol": pol},
                 device_id_type=MESH,
             )
@@ -216,8 +214,8 @@
             pltpu.make_async_remote_copy(
                 src_ref=pol_tx.at[slot, way],
                 dst_ref=pol_rx.at[slot, way],
-                send_sem=pol_send.at[slot, way],
-                recv_sem=pol_recv.at[slot, way],
+                send_sem=pol_send.at[0],
+                recv_sem=pol_recv.at[slot],
                 device_id={"tor": tor, "pol": (pol_next, pol_prev)[way]},
                 device_id_type=MESH,
             )
@@ -245,8 +243,8 @@
             pltpu.make_async_remote_copy(
                 src_ref=src.at[way],
                 dst_ref=dst.at[way],
-                send_sem=send.at[0, way],
-                recv_sem=recv.at[0, way],
+                send_sem=send.at[1],
+                recv_sem=recv.at[0],
                 device_id=(
                     {"tor": (tor_next, tor_prev)[way], "pol": pol}
                     if tor_way
@@ -297,15 +295,14 @@
         vector = [w_ref[k, c] for c in range(6)]
         result = []
         for a in range(6):
-            if k == 0:
-                loads[3 + a].wait()
+            if k == 0 and a == 0:
+                loads[3].wait()
             total = blocks[6 * a] * vector[0]
             for b in range(1, 6):
                 total = total + blocks[6 * a + b] * vector[b]
             result.append(total)
         return result
 
-    flying = []
     gram_rows = {}
 
     def product(i, j):
@@ -349,21 +346,18 @@
     state_moves = tor_copies(3) + pol_copies(3)
     for copy in tor_moves + pol_moves + state_moves:
         copy.start()
-    flying += tor_moves + pol_moves + state_moves
     for c in range(6):
         t_ref[0, c] = t[c]
     loads[2].wait()
     eta = resist[...]
     partial = local(t)
     product(0, 0)
-    for copy in pol_moves:
-        copy.wait_recv()
+    wait_bytes(edge_rx, pol_recv.at[0])
     after = [outside(1, edge_rx[1, index : index + 1, :]) for index in range(8)]
     before = [outside(0, edge_rx[0, index : index + 1, :]) for index in range(8)]
     partial = add_mixed(partial, [up_row(along_pol[1][index], after[index]) for index in range(8)], 1)
     partial = add_mixed(partial, [down_row(along_pol[0][index], before[index]) for index in range(8)], 1)
-    for copy in tor_moves:
-        copy.wait_recv()
+    wait_bytes(mix_rx, tor_recv.at[0])
     for way in range(2):
         planes = []
         for pair in range(4):
@@ -382,20 +376,18 @@
         pack_pol(k, t)
         for copy in pol_moves:
             copy.start()
-        flying += pol_moves + tor_moves
         for c in range(6):
             t_ref[k, c] = t[c]
         partial = local(t)
         for i in range(k + 1):
             product(i, k)
         if k == 1:
-            for copy in state_moves:
-                copy.wait_recv()
+            wait_bytes(tor_rx.at[3], tor_recv.at[3])
+            wait_bytes(pol_rx.at[3], pol_recv.at[3])
             for c in range(6):
                 up_ref[c] = up_row(plasma[c], pol_rx[3, 1, c : c + 1, :])
                 down_ref[c] = down_row(plasma[c], pol_rx[3, 0, c : c + 1, :])
-        for copy in pol_moves:
-            copy.wait_recv()
+        wait_bytes(pol_rx.at[k], pol_recv.at[k])
         t_up = [up_row(t[c], outside(1, pol_rx[k, 1, c : c + 1, :])) for c in range(6)]
         t_down = [down_row(t[c], outside(0, pol_rx[k, 0, c : c + 1, :])) for c in range(6)]
         f_up = flux([up_ref[c] for c in range(6)], t_up, 1)
@@ -405,8 +397,7 @@
             partial[c] = partial[c] - coefficient * (t_up[c] + t_down[c])
             if f_up[c] is not None:
                 partial[c] = partial[c] + 0.5 * (f_up[c] - f_down[c])
-        for copy in tor_moves:
-            copy.wait_recv()
+        wait_bytes(tor_rx.at[k], tor_recv.at[k])
         t_up, t_down = from_tor(k, 1), from_tor(k, 0)
         f_up = flux(from_tor(3, 1), t_up, 0)
         f_down = flux(from_tor(3, 0), t_down, 0)
@@ -437,7 +428,7 @@
         return pltpu.make_async_remote_copy(
             src_ref=sum_ref,
             dst_ref=back_ref,
-            send_sem=back_send.at[index],
+            send_sem=back_send,
             recv_sem=back_recv,
             device_id=member_at(index),
             device_id_type=MESH,
@@ -450,7 +441,7 @@
         return pltpu.make_async_remote_copy(
             src_ref=mine_ref,
             dst_ref=all_sums.at[slot[0], slot[1]],
-            send_sem=root_send.at[index],
+            send_sem=root_send,
             recv_sem=root_recv,
             device_id={"tor": index // columns, "pol": (index % columns) * GROUP + 1},
             device_id_type=MESH,
@@ -477,14 +468,18 @@
 
     mine_ref[...] = mine
 
+    def finish_halos():
+        wait_bytes(tor_rx.at[pl.ds(1, ITERS)], tor_send.at[0])
+        wait_bytes(mix_tx, tor_send.at[1])
+        wait_bytes(pol_tx.at[pl.ds(1, ITERS)], pol_send.at[0])
+        wait_bytes(edge_tx, pol_send.at[1])
+
     @pl.when(jnp.logical_not(is_root))
     def _():
         for index in order:
             to_root(index).start()
-        for copy in flying:
-            copy.wait_send()
-        for index in order:
-            to_root(index).wait_send()
+        finish_halos()
+        wait_bytes(size_ref, root_send)
         to_member(0).wait_recv()
         solve(back_ref[...])
 
@@ -497,21 +492,22 @@
             def _():
                 to_root(index).start()
 
-        for copy in flying:
-            copy.wait_send()
-        for index in order:
-
-            @pl.when(root != index)
-            def _():
-                to_root(index).wait_send()
-
+        finish_halos()
+        wait_bytes(size_ref.at[pl.ds(0, roots - 1)], root_send)
         pltpu.make_async_copy(all_sums, all_sums, root_recv).wait()
         total = tree([all_sums[m] for m in range(tors * pols // 8)])
         total = jnp.sum(total, axis=0, keepdims=True)
         sum_ref[...] = total
         for_members(lambda index: to_member(index).start())
         solve(total)
-        for_members(lambda index: to_member(index).wait_send())
+
+        @pl.when(jnp.logical_and(root != 0, root != leaders))
+        def _():
+            wait_bytes(size_ref.at[pl.ds(0, members - 1)], back_send)
+
+        @pl.when(root == leaders)
+        def _():
+            wait_bytes(size_ref.at[pl.ds(0, members - 2)], back_send)
 
 
 def combine(t_ref, weights_ref, update_ref, est_ref):
@@ -556,14 +552,15 @@
                 pltpu.VMEM((1, 128), F32),
                 pltpu.VMEM((1, 128), F32),
                 pltpu.VMEM((64, 8, 128), F32),
-                pltpu.SemaphoreType.DMA((9,)),
-                pltpu.SemaphoreType.DMA((4, 2)),
-                pltpu.SemaphoreType.DMA((4, 2)),
-                pltpu.SemaphoreType.DMA((4, 2)),
-                pltpu.SemaphoreType.DMA((4, 2)),
-                pltpu.SemaphoreType.DMA((33,)),
+                pltpu.VMEM((33, 1, 128), F32),
+                pltpu.SemaphoreType.DMA((4,)),
+                pltpu.SemaphoreType.DMA((2,)),
+                pltpu.SemaphoreType.DMA((4,)),
+                pltpu.SemaphoreType.DMA((2,)),
+                pltpu.SemaphoreType.DMA((4,)),
                 pltpu.SemaphoreType.DMA,
-                pltpu.SemaphoreType.DMA((16,)),
+                pltpu.SemaphoreType.DMA,
+                pltpu.SemaphoreType.DMA,
                 pltpu.SemaphoreType.DMA,
             ],
             compiler_params=pltpu.CompilerParams(collective_id=0, has_side_effects=True),

time: 36.1 us -> 35.4 us (0.981)
  Pallas kernels: 35.3 us -> 34.6 us
    pallas_call x1, Pallas kernels: 34.6 us -> 34 us  [shards(): pl.pallas_call(functools.partial(kernel, sizes, scale), out_shape=(pltpu....]
where the time goes in v6:
time: 35.4 us; the launch traced here: 35.2 us
  Pallas kernels  34.6 us (98%)
  between operations  0.64 us (2%)
    pallas_call x1, Pallas kernels, shards(): pl.pallas_call(functools.partial(kernel, sizes, scale), out_shape=(pltpu....  34 us

profile of v6, /device:TPU:1, one launch (start us, length us, event | category | flops | bytes accessed | tf_op | source)
XLA Modules:
  0.0 35.2 jit_solution(13089407506952403494)
XLA Ops:
  0.6 34.0 %krylov.1 = (f32[3,6,8,256]{3,2,1,0:T(8,128)S(1)}, f32[4,128]{1,0:T(4,128)S(1)}) custom-call(f32[6,8,256]{2,1,0:T(8,128)} %bitcast.8, f32[6,8,256]{2,1,0:T(8,128)} %bitcast.9, f32[8,256]{1,0:T(8,128)} %bitcast.10, f32[36,8,256]{2,1,0:T(8,128)} %bitcast.7), custom_call_target="tpu_custom_call" | custom-call | tf_op jit(solution)/shard_map/krylov/pallas_call | solution.py:530
  34.6 0.6 %combine.1 = (f32[6,8,256]{2,1,0:T(8,128)}, f32[3]{0:T(128)}) custom-call(f32[3,6,8,256]{3,2,1,0:T(8,128)S(1)} %get-tuple-element.6.t_ref, f32[4,128]{1,0:T(4,128)S(1)} %get-tuple-element.7.weights_ref), custom_call_target="tpu_custom_call" | custom-call | tf_op jit(solution)/shard_map/combine/pallas_call | solution.py:574

commit v7 on v6

--- a/solution.py
+++ b/solution.py
@@ -310,8 +310,15 @@
         for c in range(6):
             term = w_ref[i, c] * w_ref[j, c]
             total = term if total is None else total + term
-        total = total[:, 0:128] + total[:, 128:256]
-        gram_rows[(i, j)] = jnp.sum(total, axis=0, keepdims=True)
+        gram_rows[(i, j)] = total[:, 0:128] + total[:, 128:256]
+
+    narrow_lane = lax.broadcasted_iota(jnp.int32, (8, 128), 1)
+
+    def side_by_side(pairs, start):
+        for pair in pairs:
+            lanes = jnp.broadcast_to(jnp.sum(gram_rows[pair], axis=1, keepdims=True), (8, 128))
+            start = jnp.where(narrow_lane == PAIRS.index(pair), lanes, start)
+        return start
 
     def local(t):
         f = flux(own_plasma, t, 2)
@@ -381,6 +388,8 @@
         partial = local(t)
         for i in range(k + 1):
             product(i, k)
+        if k == ITERS - 1:
+            known = side_by_side([pair for pair in PAIRS if pair[1] < ITERS], jnp.zeros((8, 128), F32))
         if k == 1:
             wait_bytes(tor_rx.at[3], tor_recv.at[3])
             wait_bytes(pol_rx.at[3], pol_recv.at[3])
@@ -411,13 +420,8 @@
     for i in range(ITERS + 1):
         product(i, ITERS)
 
-    wide_lane = lax.broadcasted_iota(jnp.int32, (16, 128), 1)
-    wide_sub = lax.broadcasted_iota(jnp.int32, (16, 128), 0)
-    rows = jnp.zeros((16, 128), F32)
-    for index, pair in enumerate(PAIRS):
-        rows = jnp.where(wide_sub == index, jnp.broadcast_to(gram_rows[pair], (16, 128)), rows)
-    rows = jnp.broadcast_to(jnp.sum(rows, axis=1, keepdims=True), (16, 128))
-    mine = jnp.sum(jnp.where(wide_lane == wide_sub, rows, 0.0), axis=0, keepdims=True)
+    known = side_by_side([pair for pair in PAIRS if pair[1] == ITERS], known)
+    mine = jnp.sum(known, axis=0, keepdims=True)
 
     def tree(values):
         while len(values) > 1:

time: 35.4 us -> 35.4 us (level)
  no operation moved by 1% of the time
where the time goes in v7:
time: 35.4 us; the launch traced here: 35.2 us
  Pallas kernels  34.6 us (98%)
  between operations  0.64 us (2%)
    pallas_call x1, Pallas kernels, shards(): pl.pallas_call(functools.partial(kernel, sizes, scale), out_shape=(pltpu....  34 us

profile of v7, /device:TPU:1, one launch (start us, length us, event | category | flops | bytes accessed | tf_op | source)
XLA Modules:
  0.0 35.2 jit_solution(13407916978392733549)
XLA Ops:
  0.6 34.0 %krylov.1 = (f32[3,6,8,256]{3,2,1,0:T(8,128)S(1)}, f32[4,128]{1,0:T(4,128)S(1)}) custom-call(f32[6,8,256]{2,1,0:T(8,128)} %bitcast.8, f32[6,8,256]{2,1,0:T(8,128)} %bitcast.9, f32[8,256]{1,0:T(8,128)} %bitcast.10, f32[36,8,256]{2,1,0:T(8,128)} %bitcast.7), custom_call_target="tpu_custom_call" | custom-call | tf_op jit(solution)/shard_map/krylov/pallas_call | solution.py:534
  34.6 0.6 %combine.1 = (f32[6,8,256]{2,1,0:T(8,128)}, f32[3]{0:T(128)}) custom-call(f32[3,6,8,256]{3,2,1,0:T(8,128)S(1)} %get-tuple-element.6.t_ref, f32[4,128]{1,0:T(4,128)S(1)} %get-tuple-element.7.weights_ref), custom_call_target="tpu_custom_call" | custom-call | tf_op jit(solution)/shard_map/combine/pallas_call | solution.py:578

commit v8 on v6

--- a/solution.py
+++ b/solution.py
@@ -112,10 +112,12 @@
 
 
 def kernel(sizes, scale, plasma_hbm, right_hbm, resist_hbm, blocks_hbm, t_ref, weights_ref,
-           plasma, right, resist, blocks, w_ref, up_ref, down_ref,
+           inputs, w_ref, up_ref, down_ref,
            tor_tx, tor_rx, pol_tx, pol_rx, mix_tx, mix_rx, edge_tx, edge_rx, mine_ref, back_ref, sum_ref, all_sums, size_ref,
            load_sem, tor_send, tor_recv, pol_send, pol_recv,
            root_send, root_recv, back_send, back_recv):
+    plasma, right, blocks = inputs.at[pl.ds(0, 6)], inputs.at[pl.ds(6, 6)], inputs.at[pl.ds(12, 36)]
+    resist = inputs.at[48]
     tors, pols = sizes
     halves = 2
     width = tors // halves
@@ -160,11 +162,11 @@
         pl.semaphore_signal(barrier, inc=1, device_id={"tor": tor, "pol": neighbour}, device_id_type=MESH)
 
     loads = [
-        pltpu.make_async_copy(plasma_hbm, plasma, load_sem.at[0]),
-        pltpu.make_async_copy(right_hbm, right, load_sem.at[1]),
-        pltpu.make_async_copy(resist_hbm, resist, load_sem.at[2]),
+        pltpu.make_async_copy(plasma_hbm, plasma, load_sem),
+        pltpu.make_async_copy(right_hbm, right, load_sem),
+        pltpu.make_async_copy(resist_hbm, resist, load_sem),
     ]
-    loads.append(pltpu.make_async_copy(blocks_hbm, blocks, load_sem.at[3]))
+    loads.append(pltpu.make_async_copy(blocks_hbm, blocks, load_sem))
     for load in loads:
         load.start()
 
@@ -283,11 +285,10 @@
             planes += [both[0:8], both[8:16]]
         return planes
 
-    loads[0].wait()
+    pltpu.make_async_copy(inputs, inputs, load_sem).wait()
     own_plasma = [plasma[c] for c in range(6)]
     pack_tor(3, own_plasma)
     pack_pol(3, own_plasma)
-    loads[1].wait()
     for c in range(6):
         w_ref[0, c] = right[c]
 
@@ -295,8 +296,6 @@
         vector = [w_ref[k, c] for c in range(6)]
         result = []
         for a in range(6):
-            if k == 0 and a == 0:
-                loads[3].wait()
             total = blocks[6 * a] * vector[0]
             for b in range(1, 6):
                 total = total + blocks[6 * a + b] * vector[b]
@@ -348,7 +347,6 @@
         copy.start()
     for c in range(6):
         t_ref[0, c] = t[c]
-    loads[2].wait()
     eta = resist[...]
     partial = local(t)
     product(0, 0)
@@ -533,10 +531,7 @@
             in_specs=[hbm] * 4,
             out_specs=(vmem, vmem),
             scratch_shapes=[
-                pltpu.VMEM((6, 8, 256), F32),
-                pltpu.VMEM((6, 8, 256), F32),
-                pltpu.VMEM((8, 256), F32),
-                pltpu.VMEM((36, 8, 256), F32),
+                pltpu.VMEM((49, 8, 256), F32),
                 pltpu.VMEM((ITERS + 1, 6, 8, 256), F32),
                 pltpu.VMEM((6, 8, 256), F32),
                 pltpu.VMEM((6, 8, 256), F32),
@@ -553,7 +548,7 @@
                 pltpu.VMEM((1, 128), F32),
                 pltpu.VMEM((64, 8, 128), F32),
                 pltpu.VMEM((33, 1, 128), F32),
-                pltpu.SemaphoreType.DMA((4,)),
+                pltpu.SemaphoreType.DMA,
                 pltpu.SemaphoreType.DMA((2,)),
                 pltpu.SemaphoreType.DMA((4,)),
                 pltpu.SemaphoreType.DMA((2,)),

time: 35.4 us -> 35.4 us (level)
  no operation moved by 1% of the time
where the time goes in v8:
time: 35.4 us; the launch traced here: 35.2 us
  Pallas kernels  34.6 us (98%)
  between operations  0.64 us (2%)
    pallas_call x1, Pallas kernels, shards(): pl.pallas_call(functools.partial(kernel, sizes, scale), out_shape=(pltpu....  34 us

profile of v8, /device:TPU:1, one launch (start us, length us, event | category | flops | bytes accessed | tf_op | source)
XLA Modules:
  0.0 35.2 jit_solution(8747723019240051383)
XLA Ops:
  0.6 34.0 %krylov.1 = (f32[3,6,8,256]{3,2,1,0:T(8,128)S(1)}, f32[4,128]{1,0:T(4,128)S(1)}) custom-call(f32[6,8,256]{2,1,0:T(8,128)} %bitcast.8, f32[6,8,256]{2,1,0:T(8,128)} %bitcast.9, f32[8,256]{1,0:T(8,128)} %bitcast.10, f32[36,8,256]{2,1,0:T(8,128)} %bitcast.7), custom_call_target="tpu_custom_call" | custom-call | tf_op jit(solution)/shard_map/krylov/pallas_call | solution.py:528
  34.6 0.6 %combine.1 = (f32[6,8,256]{2,1,0:T(8,128)}, f32[3]{0:T(128)}) custom-call(f32[3,6,8,256]{3,2,1,0:T(8,128)S(1)} %get-tuple-element.6.t_ref, f32[4,128]{1,0:T(4,128)S(1)} %get-tuple-element.7.weights_ref), custom_call_target="tpu_custom_call" | custom-call | tf_op jit(solution)/shard_map/combine/pallas_call | solution.py:569
